TPU v7x, 32 devices: a whole 2x2x4 slice. The times are simulated.
32 devices in a mesh: dp: 2 (over x), context: 4 (over z), tensor: 4 (over y, core).
Axes of the slice: x: 2, y: 2, z: 4, core: 2. Of those that a mesh axis runs over, the one named last changes fastest.
Arguments:
- tokens: bfloat16 [6144, 640], P(('dp', 'context')), may hold values from -8 to 8
- seq_lengths: int32 [2, 2], P('dp'), may hold values from 1 to 2048, 3072 in all within a row
- input_gain: bfloat16 [640], P('dp'), may hold values from 0.25 to 1.75
- query_weight: bfloat16 [640, 1024], P('dp', 'tensor'), may hold values from -0.25 to 0.25
- key_weight: bfloat16 [640, 256], P('dp'), may hold values from -0.25 to 0.25
- value_weight: bfloat16 [640, 256], P('dp'), may hold values from -0.25 to 0.25
- query_gain: bfloat16 [256], P('dp'), may hold values from 0.25 to 1.75
- key_gain: bfloat16 [256], P('dp'), may hold values from 0.25 to 1.75
- output_weight: bfloat16 [1024, 640], P('tensor', 'dp'), may hold values from -0.1875 to 0.1875
- attention_gain: bfloat16 [640], P('dp'), may hold values from 0.25 to 1.75
- prefeed_gain: bfloat16 [640], P('dp'), may hold values from 0.25 to 1.75
- gate_weight: bfloat16 [640, 2048], P('dp', 'tensor'), may hold values from -0.25 to 0.25
- up_weight: bfloat16 [640, 2048], P('dp', 'tensor'), may hold values from -0.25 to 0.25
- down_weight: bfloat16 [2048, 640], P('tensor', 'dp'), may hold values from -0.125 to 0.125
- feed_gain: bfloat16 [640], P('dp'), may hold values from 0.25 to 1.75
- cotangent: bfloat16 [6144, 640], P(('dp', 'context')), may hold values from -8 to 8
Outputs:
- layer_out: bfloat16 [6144, 640], P(('dp', 'context'))
- tokens_grad: float32 [6144, 640], P(('dp', 'context'))
- input_gain_grad: float32 [640], P('dp')
- query_weight_grad: float32 [640, 1024], P('dp', 'tensor')
- key_weight_grad: float32 [640, 256], P('dp')
- value_weight_grad: float32 [640, 256], P('dp')
- query_gain_grad: float32 [256], P('dp')
- key_gain_grad: float32 [256], P('dp')
- output_weight_grad: float32 [1024, 640], P('tensor', 'dp')
- attention_gain_grad: float32 [640], P('dp')
- prefeed_gain_grad: float32 [640], P('dp')
- gate_weight_grad: float32 [640, 2048], P('dp', 'tensor')
- up_weight_grad: float32 [640, 2048], P('dp', 'tensor')
- down_weight_grad: float32 [2048, 640], P('tensor', 'dp')
- feed_gain_grad: float32 [640], P('dp')
Inputs may be any that keep to these rules, and one draw needn't show every extreme that they name: `seq_lengths`: each row lists 2 lengths that add up to 3072, none above 2048.
All inputs are finite; a program needn't handle non-finite values.
Results may differ from a plain program's by a relative error of at most 0.022.
Values may be sent and summed in bfloat16 or wider, within the bound.
No kernel may reach another device: no remote copies, remote signals or barrier semaphores. Data moves between devices by JAX's collectives and lax.ppermute only.
A program may use at most 128 MiB of HBM per device.

v0:
```python
import math

import jax
import jax.numpy as jnp
from jax import lax
from jax.sharding import PartitionSpec as P

HD = 256
LMAX = 2048
EPS = 1e-06
SCALE = 0.0625

BF = jnp.bfloat16
F32 = jnp.float32


def product(left_side, right_side):
    return jnp.dot(left_side, right_side, preferred_element_type=F32)


def product_lt(left_side, right_side):
    return lax.dot_general(
        left_side, right_side, (((0,), (0,)), ((), ())), preferred_element_type=F32
    )


def product_rt(left_side, right_side):
    return lax.dot_general(
        left_side, right_side, (((1,), (1,)), ((), ())), preferred_element_type=F32
    )


def low(values):
    return lax.reduce_precision(values, 8, 7).astype(BF)


def over_core(array):
    devices = lax.axis_size("tensor")
    return lax.ppermute(array, "tensor", [(i, i ^ 1) for i in range(devices)])


def over_pairs(array):
    devices = lax.axis_size("tensor")
    return lax.ppermute(array, "tensor", [(i, i ^ 2) for i in range(devices)])


def over_context(array, by):
    devices = lax.axis_size("context")
    pairs = [(i, i + by) for i in range(devices) if 0 <= i + by < devices]
    return lax.ppermute(array, "context", pairs)


def after(array, earlier):
    return lax.optimization_barrier((array, earlier))[0]


def ordered(place, mine, other, axis=0):
    first = place == 0
    return jnp.concatenate(
        [jnp.where(first, mine, other), jnp.where(first, other, mine)], axis=axis
    )


def pairs_sum(partial, meanwhile=None):
    short = low(partial)
    other = over_pairs(short)
    if meanwhile is not None:
        other = after(other, meanwhile)
    return short.astype(F32) + other.astype(F32)


def stacked_rows(vectors, rows):
    lanes = vectors[0].size
    place = lax.broadcasted_iota(jnp.int32, (rows, lanes), 0)
    total = jnp.zeros((rows, lanes), vectors[0].dtype)
    for number, vector in enumerate(vectors):
        wide = lax.broadcast_in_dim(vector.reshape(-1), (rows, lanes), (1,))
        total = jnp.where(place == number, wide, total)
    return total


def dp_gathered(array, axis=0):
    if lax.axis_size("dp") == 2:
        other = lax.ppermute(array, "dp", [(0, 1), (1, 0)])
        return ordered(lax.axis_index("dp"), array, other, axis)
    return lax.all_gather(array, "dp", axis=axis, tiled=True)


def dp_scattered(total):
    if lax.axis_size("dp") == 2:
        place = lax.axis_index("dp")
        rows = total.shape[0] // 2
        keep = lax.dynamic_slice_in_dim(total, place * rows, rows, 0)
        send = lax.dynamic_slice_in_dim(total, (1 - place) * rows, rows, 0)
        return keep.astype(F32) + lax.ppermute(low(send), "dp", [(0, 1), (1, 0)]).astype(F32)
    return lax.psum_scatter(low(total), "dp", scatter_dimension=0, tiled=True).astype(F32)


def sum_near(total):
    if lax.axis_size("context") != 4:
        return lax.psum(low(total), "context")
    near = lax.axis_index("context") % 2
    rows = total.shape[0] // 2
    keep = lax.dynamic_slice_in_dim(total, near * rows, rows, 0)
    send = lax.dynamic_slice_in_dim(total, (1 - near) * rows, rows, 0)
    return keep + lax.ppermute(low(send), "context", [(i, i ^ 1) for i in range(4)]).astype(F32)


def sum_far(part):
    if lax.axis_size("context") != 4:
        return part
    far = lax.axis_index("context") // 2
    rows = part.shape[0] // 2
    keep = lax.dynamic_slice_in_dim(part, far * rows, rows, 0)
    send = lax.dynamic_slice_in_dim(part, (1 - far) * rows, rows, 0)
    return low(keep + lax.ppermute(low(send), "context", [(i, i ^ 2) for i in range(4)]).astype(F32))


def spread_far(part):
    if lax.axis_size("context") != 4:
        return part
    other = lax.ppermute(part, "context", [(i, i ^ 2) for i in range(4)])
    return ordered(lax.axis_index("context") // 2, part, other)


def spread_near(part):
    if lax.axis_size("context") != 4:
        return part.astype(F32)
    other = lax.ppermute(part, "context", [(i, i ^ 1) for i in range(4)])
    return ordered(lax.axis_index("context") % 2, part, other).astype(F32)


def context_sum_small(total):
    if lax.axis_size("context") != 4:
        return lax.psum(total, "context")
    short = low(total)
    other = [
        lax.ppermute(short, "context", [(i, (i + by) % 4) for i in range(4)]).astype(F32)
        for by in (1, 2, 3)
    ]
    return (short.astype(F32) + other[1]) + (other[0] + other[2])


def partner(array, dp_turn, tensor_turn):
    count = lax.axis_size("tensor")
    pairs = [
        (i * count + j, (i ^ dp_turn) * count + (j ^ tensor_turn))
        for i in range(lax.axis_size("dp"))
        for j in range(count)
    ]
    return lax.ppermute(array, ("dp", "tensor"), pairs)


def owners_sum(total, columns):
    place = lax.axis_index("dp")
    pair = lax.axis_index("tensor") // 2
    rows = total.shape[0] // lax.axis_size("dp")
    if lax.axis_size("dp") != 2:
        total = lax.dynamic_slice_in_dim(total, pair * columns, columns, 1) + over_pairs(
            low(lax.dynamic_slice_in_dim(total, (1 - pair) * columns, columns, 1))
        ).astype(F32)
        return dp_scattered(total)

    def part(dp_turn, pair_turn):
        at = (jnp.bitwise_xor(place, dp_turn) * rows, jnp.bitwise_xor(pair, pair_turn) * columns)
        return lax.dynamic_slice(total, at, (rows, columns))

    whole = part(0, 0)
    for dp_turn, pair_turn in ((0, 1), (1, 0), (1, 1)):
        short = low(part(dp_turn, pair_turn))
        whole = whole + partner(short, dp_turn, 2 * pair_turn).astype(F32)
    return whole


def normed_of(values):
    inverse = lax.rsqrt(jnp.mean(values * values, axis=-1, keepdims=True) + EPS)
    return values * inverse, inverse


def norm_back(grad, gain, unit, inverse):
    scaled = grad * gain
    return inverse * (scaled - unit * jnp.mean(scaled * unit, axis=-1, keepdims=True))


def turned(values, cosines, sines):
    half_width = values.shape[-1] // 2
    first_half = values[..., :half_width]
    second_half = values[..., half_width:]
    return jnp.concatenate(
        [first_half * cosines - second_half * sines, second_half * cosines + first_half * sines],
        axis=-1,
    )


def local(
    tokens,
    seq_lengths,
    input_gain,
    query_weight,
    key_weight,
    value_weight,
    query_gain,
    key_gain,
    output_weight,
    attention_gain,
    prefeed_gain,
    gate_weight,
    up_weight,
    down_weight,
    feed_gain,
    cotangent,
):
    block_rows = tokens.shape[0]
    rows = block_rows // 2
    width = tokens.shape[1]
    context_place = lax.axis_index("context")
    core = lax.axis_index("tensor") % 2
    pair = lax.axis_index("tensor") // 2
    reach = min(lax.axis_size("context") - 1, (LMAX - 2) // block_rows + 1)
    dp_count = lax.axis_size("dp")
    shard = width // dp_count
    feed_width = gate_weight.shape[1]

    lanes = 2 * HD
    head_shard = HD // dp_count
    gains = jnp.concatenate(
        [
            stacked_rows([input_gain, attention_gain, prefeed_gain, feed_gain], 16),
            stacked_rows([query_gain, key_gain], 16),
        ],
        axis=1,
    )
    w_key = dp_gathered(key_weight)
    w_value = dp_gathered(value_weight)
    gain_parts = dp_gathered(gains).reshape(dp_count, 16, shard + head_shard)
    query_weight, output_weight = after((query_weight, output_weight), (w_key, w_value))
    w_query = dp_gathered(query_weight)
    w_out = dp_gathered(output_weight, axis=1)
    gate_weight, up_weight, down_weight = after(
        (gate_weight, up_weight, down_weight.T), (w_query, w_out)
    )
    w_gate, w_up, w_down = (dp_gathered(w) for w in (gate_weight, up_weight, down_weight))

    def gain_of(number, first, count):
        return gain_parts[:, number, first : first + count].reshape(1, -1).astype(F32)

    g_input, g_attention, g_prefeed, g_feed = (gain_of(i, 0, shard) for i in range(4))
    g_query, g_key = (gain_of(i, shard, head_shard) for i in (0, 1))

    stream = lax.dynamic_slice_in_dim(tokens, core * rows, rows, 0).astype(F32)
    grad_out = lax.dynamic_slice_in_dim(cotangent, core * rows, rows, 0).astype(F32)
    row_index = (
        context_place * block_rows + core * rows + lax.broadcasted_iota(jnp.int32, (rows, 1), 0)
    )
    start = jnp.zeros_like(row_index)
    begin = jnp.int32(0)
    for number in range(seq_lengths.shape[1]):
        start = jnp.where(row_index >= begin, begin, start)
        begin = begin + seq_lengths[0, number]
    frequency = jnp.exp(
        lax.broadcasted_iota(jnp.int32, (1, HD // 2), 1).astype(F32)
        * (-2.0 * math.log(1000000.0) / HD)
    )
    angles = (row_index - start).astype(F32) * frequency
    cosines, sines = lax.optimization_barrier((jnp.cos(angles), jnp.sin(angles)))
    two_cosines = jnp.concatenate([cosines, cosines], axis=0)
    two_sines = jnp.concatenate([sines, sines], axis=0)

    input_unit, input_inverse = normed_of(stream)
    normed = (input_unit * g_input).astype(BF)

    w_kv = jnp.concatenate([w_key, w_value], axis=1)
    key_value_raw = product(normed, w_kv)
    key_unit, key_inverse = normed_of(key_value_raw[:, :HD])
    kv_own = jnp.concatenate(
        [
            turned(key_unit * g_key, cosines, sines).astype(BF),
            key_value_raw[:, HD:].astype(BF),
        ],
        axis=1,
    )
    piece = rows // 2

    def piece_of(array, own=True):
        return lax.dynamic_slice_in_dim(array, (pair if own else 1 - pair) * piece, piece, 0)

    current = (kv_own[:, :HD], kv_own[:, HD:])
    arrived = [kv_own]
    for step in range(reach):
        current = (over_context(current[0], 1), over_context(current[1], 1))
        arrived.append(jnp.concatenate(current, axis=1))

    w_query, w_out = after((w_query, w_out), arrived[max(reach - 1, 0)])
    w_query_two = jnp.concatenate([w_query, over_core(w_query)], axis=1)
    w_output = jnp.concatenate([w_out, over_core(w_out)], axis=0)
    g_attention, g_prefeed, g_feed = after((g_attention, g_prefeed, g_feed), arrived[1])
    query_raw = product(normed, w_query_two)
    query_raw = jnp.concatenate([query_raw[:, :HD], query_raw[:, HD:]], axis=0)
    query_unit, query_inverse = normed_of(query_raw)
    query = turned(query_unit * g_query, two_cosines, two_sines).astype(BF)

    two_rows = jnp.concatenate([row_index, row_index], axis=0)
    two_starts = jnp.concatenate([start, start], axis=0)
    within = lax.broadcasted_iota(jnp.int32, (1, rows), 1)
    key_rows = jnp.concatenate([core * rows + within, (1 - core) * rows + within], axis=1)
    blocks = []
    kept = []
    mass = jnp.zeros((2 * rows, 1), F32)
    heads_sum = jnp.zeros((2 * rows, HD), F32)
    for step in range(reach + 1):
        both = arrived[step]
        if step == reach:
            both = after(both, (mass, heads_sum, w_output, g_attention, g_prefeed, g_feed))
        both = jnp.concatenate([both, over_core(both)], axis=0)
        key_block, value_block = both[:, :HD], both[:, HD:]
        blocks.append((key_block, value_block))
        key_index = (context_place - step) * block_rows + key_rows
        allowed = (key_index >= two_starts) & (key_index <= two_rows)
        weights = jnp.where(allowed, jnp.exp(product_rt(query, key_block) * SCALE), 0.0)
        mass = mass + jnp.sum(weights, axis=1, keepdims=True)
        weights = weights.astype(BF)
        heads_sum = heads_sum + product(weights, value_block)
        kept.append(weights)
    inverse_mass = 1.0 / mass
    heads = heads_sum * inverse_mass
    heads_low = heads.astype(BF)
    heads_wide = jnp.concatenate([heads_low[:rows], heads_low[rows:]], axis=1)
    attn_part = low(product(heads_wide, w_output))
    attn_other = over_pairs(attn_part)
    w_gate, w_up, w_down = after((w_gate, w_up, w_down), attn_part)
    w_gate_up = jnp.concatenate([w_gate, over_core(w_gate), w_up, over_core(w_up)], axis=1)
    w_down = jnp.concatenate([w_down, over_core(w_down)], axis=1)
    attn_other = after(attn_other, (w_gate_up, w_down))
    attn_sum = attn_part.astype(F32) + attn_other.astype(F32)

    attn_unit, attn_inverse = normed_of(attn_sum)
    middle = stream + attn_unit * g_attention
    middle_unit, middle_inverse = normed_of(middle)
    normed_feed = (middle_unit * g_prefeed).astype(BF)
    gate_up = product(normed_feed, w_gate_up)
    activation, activation_back = jax.vjp(
        lambda gate_part, up_part: jax.nn.gelu(gate_part, approximate=True) * up_part,
        gate_up[:, : 2 * feed_width],
        gate_up[:, 2 * feed_width :],
    )
    hidden = activation.astype(BF)
    feed_sum = pairs_sum(product_rt(hidden, w_down))
    feed_unit, feed_inverse = normed_of(feed_sum)
    layer_own = low(middle + feed_unit * g_feed)
    layer_out = ordered(core, layer_own, over_core(layer_own))

    grad_gfeed = jnp.sum(grad_out * feed_unit, axis=0, keepdims=True)
    grad_feed = norm_back(grad_out, g_feed, feed_unit, feed_inverse).astype(BF)
    grad_gate_full, grad_up_full = activation_back(product(grad_feed, w_down))
    grad_gate_up = jnp.concatenate([grad_gate_full.astype(BF), grad_up_full.astype(BF)], axis=1)
    def shared(total, own, other):
        mine = jnp.concatenate([total[:, a:b] for a, b in own], axis=1)
        theirs = jnp.concatenate([total[:, a:b] for a, b in other], axis=1)
        return mine, low(theirs)

    parts_down = shared(
        product_lt(grad_feed, hidden), [(0, feed_width)], [(feed_width, 2 * feed_width)]
    )
    whole_down = parts_down[0] + over_core(parts_down[1]).astype(F32)
    feed_part = low(product_rt(grad_gate_up, w_gate_up))
    feed_other = over_pairs(feed_part)
    parts_gate_up = shared(
        product_lt(*after((normed_feed, grad_gate_up), feed_part)),
        [(0, feed_width), (2 * feed_width, 3 * feed_width)],
        [(feed_width, 2 * feed_width), (3 * feed_width, 4 * feed_width)],
    )
    whole_gate_up = parts_gate_up[0] + over_core(parts_gate_up[1]).astype(F32)
    shard_down = dp_scattered(whole_down)
    feed_other = after(feed_other, (whole_gate_up, shard_down, layer_out))
    grad_normed_feed = feed_part.astype(F32) + feed_other.astype(F32)
    shard_gate_up = dp_scattered(whole_gate_up)
    near_down = sum_near(shard_down)

    grad_gprefeed = jnp.sum(grad_normed_feed * middle_unit, axis=0, keepdims=True)
    grad_middle = grad_out + norm_back(grad_normed_feed, g_prefeed, middle_unit, middle_inverse)
    grad_gattention = jnp.sum(grad_middle * attn_unit, axis=0, keepdims=True)
    grad_attn = norm_back(grad_middle, g_attention, attn_unit, attn_inverse).astype(BF)

    grad_heads_wide = product_rt(grad_attn, w_output)
    grad_heads = jnp.concatenate([grad_heads_wide[:, :HD], grad_heads_wide[:, HD:]], axis=0)
    grad_heads_low = (grad_heads * inverse_mass).astype(BF)
    row_dots = jnp.sum(grad_heads * heads, axis=1, keepdims=True) * inverse_mass
    grad_query = jnp.zeros((2 * rows, HD), F32)
    block_grads = {}
    for step in range(reach, -1, -1):
        key_block, value_block = blocks[step]
        weights = kept[step]
        if step == reach - 1:
            weights = after(weights, (near_down, block_grads[reach]))
            far_down = sum_far(near_down)
        if step == reach - 2:
            weights = after(weights, (far_down, block_grads[reach - 1]))
            all_down = spread_far(far_down)
        if step == 0:
            weights = after(weights, (shard_gate_up, all_down, block_grads[1]))
            near_gate_up = sum_near(shard_gate_up)
        grad_scores = (
            weights.astype(F32) * (product_rt(grad_heads_low, value_block) - row_dots)
        ).astype(BF)
        block_grads[step] = jnp.concatenate(
            [product_lt(grad_scores, query) * SCALE, product_lt(weights, grad_heads_low)], axis=1
        )
        grad_query = grad_query + product(grad_scores, key_block)
    grad_query_turned = turned(grad_query * SCALE, two_cosines, -two_sines)
    grad_gquery = jnp.sum(grad_query_turned * query_unit, axis=0, keepdims=True)
    grad_query_raw = norm_back(grad_query_turned, g_query, query_unit, query_inverse).astype(BF)
    grad_query_wide = jnp.concatenate([grad_query_raw[:rows], grad_query_raw[rows:]], axis=1)
    grad_normed_query = product_rt(grad_query_wide, w_query_two)
    parts_qo = shared(
        jnp.concatenate(
            [product_lt(normed, grad_query_wide), product_lt(grad_attn, heads_wide)], axis=1
        ),
        [(0, HD), (2 * HD, 3 * HD)],
        [(HD, 2 * HD), (3 * HD, 4 * HD)],
    )
    whole_qo = parts_qo[0] + over_core(parts_qo[1]).astype(F32)

    def group_sum(group, first_due, then_due):
        theirs = over_core(jnp.concatenate([low(block_grads[s][rows:]) for s in group], axis=0))
        if first_due is not None:
            theirs = after(theirs, first_due)
        mine = jnp.concatenate([block_grads[s][:rows] for s in group], axis=0) + theirs.astype(F32)
        mine = mine.reshape(len(group), rows, lanes)
        keep = lax.dynamic_slice_in_dim(mine, pair * piece, piece, 1)
        send = low(lax.dynamic_slice_in_dim(mine, (1 - pair) * piece, piece, 1))
        other = over_pairs(send)
        if then_due is not None:
            other = after(other, then_due)
        return keep + other.astype(F32)

    far_group = list(range(reach, 1, -1))
    near_group = [1, 0]
    far_sums = group_sum(far_group, near_gate_up, whole_qo)
    far_gate_up = sum_far(near_gate_up)
    shard_qo = dp_scattered(whole_qo)
    far_parts = [
        over_context(low(far_sums[number]), -step) for number, step in enumerate(far_group)
    ]
    near_sums = group_sum(near_group, far_gate_up, far_parts[0])
    near_part = over_context(low(near_sums[0]), -1)
    all_gate_up = spread_far(far_gate_up)
    grad_normed_query_low = low(after(grad_normed_query, near_sums))
    far_parts, near_part = after((far_parts, near_part), (shard_qo, all_gate_up))
    grad_kv = near_sums[1] + near_part.astype(F32)
    for part in far_parts:
        grad_kv = grad_kv + part.astype(F32)
    grad_normed = grad_normed_query_low.astype(F32) + over_pairs(grad_normed_query_low).astype(F32)

    piece_unit = piece_of(key_unit)
    grad_key_turned = turned(grad_kv[:, :HD], piece_of(cosines), -piece_of(sines))
    grad_gkey = jnp.sum(grad_key_turned * piece_unit, axis=0, keepdims=True)
    grad_key_raw = norm_back(grad_key_turned, g_key, piece_unit, piece_of(key_inverse)).astype(BF)
    grad_kv_raw = jnp.concatenate([grad_key_raw, grad_kv[:, HD:].astype(BF)], axis=1)
    grad_normed_kv = low(product_rt(grad_kv_raw, w_kv))
    grad_ginput = jnp.sum(grad_normed_query * input_unit, axis=0, keepdims=True) + jnp.sum(
        grad_normed_kv.astype(F32) * piece_of(input_unit), axis=0, keepdims=True
    )

    once = jnp.where(pair == 0, 1.0, 0.0).astype(F32)
    long_grads = [
        grad_ginput, grad_gattention * once, grad_gprefeed * once, grad_gfeed * once
    ]
    gain_rows = [
        jnp.pad(
            jnp.concatenate(
                [
                    stacked_rows([g[:, i * shard : (i + 1) * shard] for g in long_grads], 16),
                    stacked_rows(
                        [
                            g[:, i * head_shard : (i + 1) * head_shard]
                            for g in (grad_gquery, grad_gkey)
                        ],
                        16,
                    ),
                ],
                axis=1,
            ),
            ((0, 0), (0, lanes - shard - head_shard)),
        )
        for i in range(dp_count)
    ]
    grad_w_kv = product_lt(piece_of(normed), grad_kv_raw)
    small = jnp.concatenate(
        [
            part
            for i in range(dp_count)
            for part in (
                grad_w_kv[i * shard : (i + 1) * shard],
                gain_rows[i],
            )
        ],
        axis=0,
    )
    columns = lanes // 2
    send = low(lax.dynamic_slice_in_dim(small, (1 - core) * columns, columns, 1))
    other = over_core(send)
    near_qo = sum_near(after(shard_qo, send))
    grad_normed_kv = after(grad_normed_kv, send)
    small = lax.dynamic_slice_in_dim(small, core * columns, columns, 1) + other.astype(F32)
    far_qo = sum_far(after(near_qo, small))
    small = owners_sum(small, columns // 2)
    other = over_pairs(grad_normed_kv)
    grad_normed = grad_normed + ordered(pair, grad_normed_kv, other).astype(F32)
    tokens_own = grad_middle + norm_back(grad_normed, g_input, input_unit, input_inverse)
    tokens_other = over_core(tokens_own)
    small = after(small, far_qo)
    total_gate_up = spread_near(all_gate_up)
    all_qo = spread_far(far_qo)
    small = low(context_sum_small(small))
    total_qo = spread_near(all_qo)
    total_down = spread_near(all_down)
    tokens_grad = ordered(core, tokens_own, tokens_other)
    over_both = partner(small, 0, 3)
    other_core = over_core(small)
    small = ordered(pair, small, over_pairs(small), axis=1)
    small = ordered(core, small, ordered(pair, other_core, over_both, axis=1), axis=1).astype(F32)

    return (
        layer_out,
        tokens_grad,
        small[shard, :shard],
        total_qo[:, :HD],
        small[:shard, :HD],
        small[:shard, HD:],
        small[shard, shard : shard + head_shard],
        small[shard + 1, shard : shard + head_shard],
        total_qo[:, HD:].T,
        small[shard + 1, :shard],
        small[shard + 2, :shard],
        total_gate_up[:, :feed_width],
        total_gate_up[:, feed_width:],
        total_down.T,
        small[shard + 3, :shard],
    )


def solution(mesh):
    placed = (
        P(("dp", "context"), None),
        P("dp", None),
        P("dp"),
        P("dp", "tensor"),
        P("dp", None),
        P("dp", None),
        P("dp"),
        P("dp"),
        P("tensor", "dp"),
        P("dp"),
        P("dp"),
        P("dp", "tensor"),
        P("dp", "tensor"),
        P("tensor", "dp"),
        P("dp"),
        P(("dp", "context"), None),
    )
    return jax.shard_map(
        local,
        mesh=mesh,
        in_specs=placed,
        out_specs=(
            P(("dp", "context"), None),
            P(("dp", "context"), None),
            P("dp"),
            P("dp", "tensor"),
            P("dp", None),
            P("dp", None),
            P("dp"),
            P("dp"),
            P("tensor", "dp"),
            P("dp"),
            P("dp"),
            P("dp", "tensor"),
            P("dp", "tensor"),
            P("tensor", "dp"),
            P("dp"),
        ),
        check_vma=False,
    )
```

profile of v0, /device:TPU:0, one launch (start us, length us, event | category | flops | bytes accessed | tf_op | source)
XLA Modules:
  0.0 266.4 jit_solution(17929375023011284938)
XLA Ops:
  2.5 2.9 %collective-permute-start = (bf16[16,448]{1,0:T(8,128)(2,1)S(1)}, bf16[16,448]{1,0:T(8,128)(2,1)S(1)}, u32[]{:S(2)}, u32[]{:S(2)}) collective-permute-start(bf16[16,448]{1,0:T(8,128)(2,1)S(1)} %pad_maximum_fusion.46), channel_id=1, source_target_pairs={{0,16},{16,0},{1,17},{17,1},{2,18},{18,2},{3,19},{19,3},{4,20},{20... | collective-permute-start | bytes 43016 | tf_op jit(solution)/shard_map/ppermute | solution.py:84
  5.5 1.9 collective-permute-start.2
  7.5 1.9 collective-permute-start.4
  13.2 3.0 %collective-permute-done.2 = bf16[320,256]{1,0:T(8,128)(2,1)S(1)} collective-permute-done((bf16[320,256]{1,0:T(8,128)(2,1)}, bf16[320,256]{1,0:T(8,128)(2,1)S(1)}, u32[]{:S(2)}, u32[]{:S(2)}) %collective-permute-start.2) | collective-permute-done | bytes 163872 | tf_op jit(solution)/shard_map/ppermute | solution.py:84
  18.3 3.7 %collective-permute-start.5 = (bf16[384,256]{1,0:T(8,128)(2,1)S(1)}, bf16[384,256]{1,0:T(8,128)(2,1)S(1)}, u32[]{:S(2)}, u32[]{:S(2)}) collective-permute-start(bf16[384,256]{1,0:T(8,128)(2,1)S(1)} %pad_maximum_fusion.32), channel_id=1, source_target_pairs={{0,4},{4,8},{8,12},{1,5},{5,9},{9,13},{2,6},{6,10},{10,14},{3,7},{... | collective-permute-start | bytes 589832 | tf_op jit(solution)/shard_map/ppermute | solution.py:50
  21.9 3.5 %collective-permute-start.7 = (bf16[384,256]{1,0:T(8,128)(2,1)S(1)}, bf16[384,256]{1,0:T(8,128)(2,1)S(1)}, u32[]{:S(2)}, u32[]{:S(2)}) collective-permute-start(bf16[384,256]{1,0:T(8,128)(2,1)S(1)} %slice.600), channel_id=1, source_target_pairs={{0,4},{4,8},{8,12},{1,5},{5,9},{9,13},{2,6},{6,10},{10,14},{3,7},{... | collective-permute-start | bytes 589832 | tf_op jit(solution)/shard_map/ppermute | solution.py:50
  26.3 1.6 collective-permute-start.18
  28.8 7.3 %collective-permute-done.19 = bf16[320,512]{1,0:T(8,128)(2,1)S(1)} collective-permute-done((bf16[320,512]{1,0:T(8,128)(2,1)S(1)}, bf16[320,512]{1,0:T(8,128)(2,1)S(1)}, u32[]{:S(2)}, u32[]{:S(2)}) %collective-permute-start.19) | collective-permute-done | bytes 327712 | tf_op jit(solution)/shard_map/ppermute | solution.py:84
  36.1 3.4 %collective-permute-start.6 = (bf16[384,256]{1,0:T(8,128)(2,1)S(1)}, bf16[384,256]{1,0:T(8,128)(2,1)S(1)}, u32[]{:S(2)}, u32[]{:S(2)}) collective-permute-start(bf16[384,256]{1,0:T(8,128)(2,1)S(1)} %collective-permute-done.5), channel_id=1, source_target_pairs={{0,4},{4,8},{8,12},{1,5},{5,9},{9,13},{2,6},{6,10},{10,14},{3,7},{... | collective-permute-start | bytes 589832 | tf_op jit(solution)/shard_map/ppermute | solution.py:50
  39.6 3.5 %collective-permute-done.18 = bf16[320,512]{1,0:T(8,128)(2,1)S(1)} collective-permute-done((bf16[320,512]{1,0:T(8,128)(2,1)S(1)}, bf16[320,512]{1,0:T(8,128)(2,1)S(1)}, u32[]{:S(2)}, u32[]{:S(2)}) %collective-permute-start.18) | collective-permute-done | bytes 327712 | tf_op jit(solution)/shard_map/ppermute | solution.py:84
  43.1 3.4 %collective-permute-start.8 = (bf16[384,256]{1,0:T(8,128)(2,1)S(1)}, bf16[384,256]{1,0:T(8,128)(2,1)S(1)}, u32[]{:S(2)}, u32[]{:S(2)}) collective-permute-start(bf16[384,256]{1,0:T(8,128)(2,1)S(1)} %collective-permute-done.7), channel_id=1, source_target_pairs={{0,4},{4,8},{8,12},{1,5},{5,9},{9,13},{2,6},{6,10},{10,14},{3,7},{... | collective-permute-start | bytes 589832 | tf_op jit(solution)/shard_map/ppermute | solution.py:50
  46.9 2.8 %collective-permute-done.8 = bf16[384,256]{1,0:T(8,128)(2,1)S(1)} collective-permute-done((bf16[384,256]{1,0:T(8,128)(2,1)S(1)}, bf16[384,256]{1,0:T(8,128)(2,1)S(1)}, u32[]{:S(2)}, u32[]{:S(2)}) %collective-permute-start.8) | collective-permute-done | bytes 196640 | tf_op jit(solution)/shard_map/ppermute | solution.py:50
  49.8 4.4 %collective-permute-start.13 = (bf16[384,256]{1,0:T(8,128)(2,1)S(1)}, bf16[384,256]{1,0:T(8,128)(2,1)S(1)}, u32[]{:S(2)}, u32[]{:S(2)}) collective-permute-start(bf16[384,256]{1,0:T(8,128)(2,1)S(1)} %collective-permute-done.6), channel_id=1, source_target_pairs={{0,4},{4,8},{8,12},{1,5},{5,9},{9,13},{2,6},{6,10},{10,14},{3,7},{... | collective-permute-start | bytes 589832 | tf_op jit(solution)/shard_map/ppermute | solution.py:50
  54.2 2.1 collective-permute-start.14
  56.7 2.7 %collective-permute-done.13 = bf16[384,256]{1,0:T(8,128)(2,1)S(1)} collective-permute-done((bf16[384,256]{1,0:T(8,128)(2,1)S(1)}, bf16[384,256]{1,0:T(8,128)(2,1)S(1)}, u32[]{:S(2)}, u32[]{:S(2)}) %collective-permute-start.13) | collective-permute-done | bytes 196640 | tf_op jit(solution)/shard_map/ppermute | solution.py:50
  59.4 3.8 %collective-permute-done.14 = bf16[384,256]{1,0:T(8,128)(2,1)S(1)} collective-permute-done((bf16[384,256]{1,0:T(8,128)(2,1)S(1)}, bf16[384,256]{1,0:T(8,128)(2,1)S(1)}, u32[]{:S(2)}, u32[]{:S(2)}) %collective-permute-start.14) | collective-permute-done | bytes 196640 | tf_op jit(solution)/shard_map/ppermute | solution.py:50
  75.6 1.6 collective-permute-start.17
  82.1 1.6 constant_dynamic-update-slice_fusion.14
  83.7 5.2 %collective-permute-done.17 = bf16[384,640]{1,0:T(8,128)(2,1)S(1)} collective-permute-done((bf16[384,640]{1,0:T(8,128)(2,1)S(1)}, bf16[384,640]{1,0:T(8,128)(2,1)S(1)}, u32[]{:S(2)}, u32[]{:S(2)}) %collective-permute-start.17) | collective-permute-done | bytes 491552 | tf_op jit(solution)/shard_map/ppermute | solution.py:44
  94.5 1.6 fusion.17
  97.8 11.1 %collective-permute-done.24 = bf16[384,640]{1,0:T(8,128)(2,1)} collective-permute-done((bf16[384,640]{1,0:T(8,128)(2,1)}, bf16[384,640]{1,0:T(8,128)(2,1)}, u32[]{:S(2)}, u32[]{:S(2)}) %collective-permute-start.24) | collective-permute-done | bytes 491552 | tf_op jit(solution)/shard_map/ppermute | solution.py:44
  110.3 1.9 fusion.25
  112.2 2.0 fusion.23
  116.0 1.7 fusion.7
  117.9 1.6 copy-done.22
  121.2 1.6 collective-permute-start.26
  122.7 1.6 fusion.116
  126.3 9.7 %collective-permute-done.29 = bf16[320,512]{1,0:T(8,128)(2,1)S(1)} collective-permute-done((bf16[320,512]{1,0:T(8,128)(2,1)S(1)}, bf16[320,512]{1,0:T(8,128)(2,1)S(1)}, u32[]{:S(2)}, u32[]{:S(2)}) %collective-permute-start.29) | collective-permute-done | bytes 327712 | tf_op jit(solution)/shard_map/ppermute | solution.py:95
  136.1 2.5 collective-permute-start.30
  138.8 3.6 %collective-permute-done.30 = bf16[160,512]{1,0:T(8,128)(2,1)S(1)} collective-permute-done((bf16[160,512]{1,0:T(8,128)(2,1)S(1)}, bf16[160,512]{1,0:T(8,128)(2,1)S(1)}, u32[]{:S(2)}, u32[]{:S(2)}) %collective-permute-start.30) | collective-permute-done | bytes 163872 | tf_op jit(solution)/shard_map/ppermute | solution.py:106
  142.4 1.5 collective-permute-start.31
  145.0 2.8 %collective-permute-done.31 = bf16[80,512]{1,0:T(8,128)(2,1)S(1)} collective-permute-done((bf16[80,512]{1,0:T(8,128)(2,1)S(1)}, bf16[80,512]{1,0:T(8,128)(2,1)S(1)}, u32[]{:S(2)}, u32[]{:S(2)}) %collective-permute-start.31) | collective-permute-done | bytes 81952 | tf_op jit(solution)/shard_map/ppermute | solution.py:116
  165.9 2.7 %collective-permute-done.32 = bf16[320,1024]{1,0:T(8,128)(2,1)S(1)} collective-permute-done((bf16[320,1024]{1,0:T(8,128)(2,1)S(1)}, bf16[320,1024]{1,0:T(8,128)(2,1)S(1)}, u32[]{:S(2)}, u32[]{:S(2)}) %collective-permute-start.32) | collective-permute-done | bytes 655392 | tf_op jit(solution)/shard_map/ppermute | solution.py:95
  179.3 2.8 %collective-permute-start.36 = (bf16[80,1024]{1,0:T(8,128)(2,1)S(1)}, bf16[80,1024]{1,0:T(8,128)(2,1)S(1)}, u32[]{:S(2)}, u32[]{:S(2)}) collective-permute-start(bf16[80,1024]{1,0:T(8,128)(2,1)S(1)} %reduce-precision_convert_fusion.11), channel_id=1, source_target_pairs={{0,8},{4,12},{8,0},{12,4},{1,9},{5,13},{9,1},{13,5},{2,10},{6,14},... | collective-permute-start | bytes 491528 | tf_op jit(solution)/shard_map/ppermute | solution.py:116
  183.1 5.3 %collective-permute-done.36 = bf16[80,1024]{1,0:T(8,128)(2,1)S(1)} collective-permute-done((bf16[80,1024]{1,0:T(8,128)(2,1)S(1)}, bf16[80,1024]{1,0:T(8,128)(2,1)S(1)}, u32[]{:S(2)}, u32[]{:S(2)}) %collective-permute-start.36) | collective-permute-done | bytes 163872 | tf_op jit(solution)/shard_map/ppermute | solution.py:116
  190.3 8.1 %collective-permute-done.46 = bf16[80,1024]{1,0:T(8,128)(2,1)S(1)} collective-permute-done((bf16[80,1024]{1,0:T(8,128)(2,1)S(1)}, bf16[80,1024]{1,0:T(8,128)(2,1)S(1)}, u32[]{:S(2)}, u32[]{:S(2)}) %collective-permute-start.46) | collective-permute-done | bytes 163872 | tf_op jit(solution)/shard_map/ppermute | solution.py:122
  201.9 12.7 %collective-permute-done.63 = bf16[160,1024]{1,0:T(8,128)(2,1)S(1)} collective-permute-done((bf16[160,1024]{1,0:T(8,128)(2,1)S(1)}, bf16[160,1024]{1,0:T(8,128)(2,1)S(1)}, u32[]{:S(2)}, u32[]{:S(2)}) %collective-permute-start.63) | collective-permute-done | bytes 327712 | tf_op jit(solution)/shard_map/ppermute | solution.py:129
  215.1 1.6 collective-permute-start.44
  218.3 4.8 %collective-permute-done.44 = bf16[192,512]{1,0:T(8,128)(2,1)S(1)} collective-permute-done((bf16[192,512]{1,0:T(8,128)(2,1)S(1)}, bf16[192,512]{1,0:T(8,128)(2,1)S(1)}, u32[]{:S(2)}, u32[]{:S(2)}) %collective-permute-start.44) | collective-permute-done | bytes 196640 | tf_op jit(solution)/shard_map/ppermute | solution.py:50
  227.6 3.8 %collective-permute-done.53 = bf16[160,512]{1,0:T(8,128)(2,1)S(1)} collective-permute-done((bf16[160,512]{1,0:T(8,128)(2,1)S(1)}, bf16[160,512]{1,0:T(8,128)(2,1)S(1)}, u32[]{:S(2)}, u32[]{:S(2)}) %collective-permute-start.53) | collective-permute-done | bytes 163872 | tf_op jit(solution)/shard_map/ppermute | solution.py:106
  231.4 2.9 %collective-permute-done.47 = bf16[192,640]{1,0:T(8,128)(2,1)S(1)} collective-permute-done((bf16[192,640]{1,0:T(8,128)(2,1)S(1)}, bf16[192,640]{1,0:T(8,128)(2,1)S(1)}, u32[]{:S(2)}, u32[]{:S(2)}) %collective-permute-start.47) | collective-permute-done | bytes 245792 | tf_op jit(solution)/shard_map/ppermute | solution.py:44
  238.3 2.3 collective-permute-start.52
  242.9 1.8 collective-permute-done.52
  244.8 1.6 collective-permute-start.55
  246.5 2.4 collective-permute-start.56
  250.3 4.1 %collective-permute-done.55 = bf16[336,128]{1,0:T(8,128)(2,1)S(1)} collective-permute-done((bf16[336,128]{1,0:T(8,128)(2,1)S(1)}, bf16[336,128]{1,0:T(8,128)(2,1)S(1)}, u32[]{:S(2)}, u32[]{:S(2)}) %collective-permute-start.55) | collective-permute-done | bytes 86048 | tf_op jit(solution)/shard_map/ppermute | solution.py:138
  257.0 1.8 collective-permute-start.60
  259.6 1.7 collective-permute-done.60
  (494 shorter events, 98.7 us)
Async XLA Ops:
  2.5 10.0 %collective-permute-start = (bf16[16,448]{1,0:T(8,128)(2,1)S(1)}, bf16[16,448]{1,0:T(8,128)(2,1)S(1)}, u32[]{:S(2)}, u32[]{:S(2)}) collective-permute-start(bf16[16,448]{1,0:T(8,128)(2,1)S(1)} %pad_maximum_fusion.46), channel_id=1, source_target_pairs={{0,16},{16,0},{1,17},{17,1},{2,18},{18,2},{3,19},{19,3},{4,20},{20... | collective-permute-start | bytes 43016 | tf_op jit(solution)/shard_map/ppermute | solution.py:84
  5.4 7.8 %collective-permute-start.1 = (bf16[320,256]{1,0:T(8,128)(2,1)}, bf16[320,256]{1,0:T(8,128)(2,1)S(1)}, u32[]{:S(2)}, u32[]{:S(2)}) collective-permute-start(bf16[320,256]{1,0:T(8,128)(2,1)} %param.20), channel_id=1, source_target_pairs={{0,16},{16,0},{1,17},{17,1},{2,18},{18,2},{3,19},{19,3},{4,20},{20... | collective-permute-start | bytes 491528 | tf_op jit(solution)/shard_map/ppermute | solution.py:84
  5.5 10.8 %collective-permute-start.2 = (bf16[320,256]{1,0:T(8,128)(2,1)}, bf16[320,256]{1,0:T(8,128)(2,1)S(1)}, u32[]{:S(2)}, u32[]{:S(2)}) collective-permute-start(bf16[320,256]{1,0:T(8,128)(2,1)} %param.21), channel_id=1, source_target_pairs={{0,16},{16,0},{1,17},{17,1},{2,18},{18,2},{3,19},{19,3},{4,20},{20... | collective-permute-start | bytes 491528 | tf_op jit(solution)/shard_map/ppermute | solution.py:84
  7.4 18.0 %collective-permute-start.3 = (bf16[320,256]{1,0:T(8,128)(2,1)}, bf16[320,256]{1,0:T(8,128)(2,1)S(1)}, u32[]{:S(2)}, u32[]{:S(2)}) collective-permute-start(bf16[320,256]{1,0:T(8,128)(2,1)} %param.19), channel_id=1, source_target_pairs={{0,16},{16,0},{1,17},{17,1},{2,18},{18,2},{3,19},{19,3},{4,20},{20... | collective-permute-start | bytes 491528 | tf_op jit(solution)/shard_map/ppermute | solution.py:84
  7.5 18.0 %collective-permute-start.4 = (bf16[256,320]{0,1:T(8,128)(2,1)}, bf16[256,320]{0,1:T(8,128)(2,1)S(1)}, u32[]{:S(2)}, u32[]{:S(2)}) collective-permute-start(bf16[256,320]{0,1:T(8,128)(2,1)} %param.24), channel_id=1, source_target_pairs={{0,16},{16,0},{1,17},{17,1},{2,18},{18,2},{3,19},{19,3},{4,20},{20... | collective-permute-start | bytes 491528 | tf_op jit(solution)/shard_map/ppermute | solution.py:84
  18.3 9.6 %collective-permute-start.5 = (bf16[384,256]{1,0:T(8,128)(2,1)S(1)}, bf16[384,256]{1,0:T(8,128)(2,1)S(1)}, u32[]{:S(2)}, u32[]{:S(2)}) collective-permute-start(bf16[384,256]{1,0:T(8,128)(2,1)S(1)} %pad_maximum_fusion.32), channel_id=1, source_target_pairs={{0,4},{4,8},{8,12},{1,5},{5,9},{9,13},{2,6},{6,10},{10,14},{3,7},{... | collective-permute-start | bytes 589832 | tf_op jit(solution)/shard_map/ppermute | solution.py:50
  21.9 6.8 %collective-permute-start.7 = (bf16[384,256]{1,0:T(8,128)(2,1)S(1)}, bf16[384,256]{1,0:T(8,128)(2,1)S(1)}, u32[]{:S(2)}, u32[]{:S(2)}) collective-permute-start(bf16[384,256]{1,0:T(8,128)(2,1)S(1)} %slice.600), channel_id=1, source_target_pairs={{0,4},{4,8},{8,12},{1,5},{5,9},{9,13},{2,6},{6,10},{10,14},{3,7},{... | collective-permute-start | bytes 589832 | tf_op jit(solution)/shard_map/ppermute | solution.py:50
  25.6 10.5 %collective-permute-start.19 = (bf16[320,512]{1,0:T(8,128)(2,1)S(1)}, bf16[320,512]{1,0:T(8,128)(2,1)S(1)}, u32[]{:S(2)}, u32[]{:S(2)}) collective-permute-start(bf16[320,512]{1,0:T(8,128)(2,1)S(1)} %copy-done.58), channel_id=1, source_target_pairs={{0,16},{16,0},{1,17},{17,1},{2,18},{18,2},{3,19},{19,3},{4,20},{20... | collective-permute-start | bytes 983048 | tf_op jit(solution)/shard_map/ppermute | solution.py:84
  26.2 30.2 %collective-permute-start.10 = (bf16[384,512]{1,0:T(8,128)(2,1)S(1)}, bf16[384,512]{1,0:T(8,128)(2,1)S(1)}, u32[]{:S(2)}, u32[]{:S(2)}) collective-permute-start(bf16[384,512]{1,0:T(8,128)(2,1)S(1)} %pad_maximum_fusion.21), channel_id=1, source_target_pairs={{0,1},{1,0},{2,3},{3,2},{4,5},{5,4},{6,7},{7,6},{8,9},{9,8},{10,11... | collective-permute-start | bytes 1179656 | tf_op jit(solution)/shard_map/ppermute | solution.py:39
  26.3 16.8 %collective-permute-start.18 = (bf16[320,512]{1,0:T(8,128)(2,1)S(1)}, bf16[320,512]{1,0:T(8,128)(2,1)S(1)}, u32[]{:S(2)}, u32[]{:S(2)}) collective-permute-start(bf16[320,512]{1,0:T(8,128)(2,1)S(1)} %copy-done.59), channel_id=1, source_target_pairs={{0,16},{16,0},{1,17},{17,1},{2,18},{18,2},{3,19},{19,3},{4,20},{20... | collective-permute-start | bytes 983048 | tf_op jit(solution)/shard_map/ppermute | solution.py:84
  27.9 18.9 %collective-permute-start.20 = (bf16[320,512]{1,0:T(8,128)(2,1)S(1)}, bf16[320,512]{1,0:T(8,128)(2,1)S(1)}, u32[]{:S(2)}, u32[]{:S(2)}) collective-permute-start(bf16[320,512]{1,0:T(8,128)(2,1)S(1)} %bitcast.88), channel_id=1, source_target_pairs={{0,16},{16,0},{1,17},{17,1},{2,18},{18,2},{3,19},{19,3},{4,20},{20... | collective-permute-start | bytes 983048 | tf_op jit(solution)/shard_map/ppermute | solution.py:84
  28.7 36.3 %collective-permute-start.11 = (bf16[384,512]{1,0:T(8,128)(2,1)S(1)}, bf16[384,512]{1,0:T(8,128)(2,1)S(1)}, u32[]{:S(2)}, u32[]{:S(2)}) collective-permute-start(bf16[384,512]{1,0:T(8,128)(2,1)S(1)} %constant_dynamic-update-slice_fusion.8), channel_id=1, source_target_pairs={{0,1},{1,0},{2,3},{3,2},{4,5},{5,4},{6,7},{7,6},{8,9},{9,8},{10,11... | collective-permute-start | bytes 1179656 | tf_op jit(solution)/shard_map/ppermute | solution.py:39
  36.1 10.8 %collective-permute-start.6 = (bf16[384,256]{1,0:T(8,128)(2,1)S(1)}, bf16[384,256]{1,0:T(8,128)(2,1)S(1)}, u32[]{:S(2)}, u32[]{:S(2)}) collective-permute-start(bf16[384,256]{1,0:T(8,128)(2,1)S(1)} %collective-permute-done.5), channel_id=1, source_target_pairs={{0,4},{4,8},{8,12},{1,5},{5,9},{9,13},{2,6},{6,10},{10,14},{3,7},{... | collective-permute-start | bytes 589832 | tf_op jit(solution)/shard_map/ppermute | solution.py:50
  49.7 13.5 %collective-permute-start.9 = (bf16[640,256]{1,0:T(8,128)(2,1)S(1)}, bf16[640,256]{1,0:T(8,128)(2,1)S(1)}, u32[]{:S(2)}, u32[]{:S(2)}) collective-permute-start(bf16[640,256]{1,0:T(8,128)(2,1)S(1)} %pad_maximum_fusion.25), channel_id=1, source_target_pairs={{0,1},{1,0},{2,3},{3,2},{4,5},{5,4},{6,7},{7,6},{8,9},{9,8},{10,11... | collective-permute-start | bytes 983048 | tf_op jit(solution)/shard_map/ppermute | solution.py:39
  49.8 9.6 %collective-permute-start.13 = (bf16[384,256]{1,0:T(8,128)(2,1)S(1)}, bf16[384,256]{1,0:T(8,128)(2,1)S(1)}, u32[]{:S(2)}, u32[]{:S(2)}) collective-permute-start(bf16[384,256]{1,0:T(8,128)(2,1)S(1)} %collective-permute-done.6), channel_id=1, source_target_pairs={{0,4},{4,8},{8,12},{1,5},{5,9},{9,13},{2,6},{6,10},{10,14},{3,7},{... | collective-permute-start | bytes 589832 | tf_op jit(solution)/shard_map/ppermute | solution.py:50
  54.2 9.0 %collective-permute-start.14 = (bf16[384,256]{1,0:T(8,128)(2,1)S(1)}, bf16[384,256]{1,0:T(8,128)(2,1)S(1)}, u32[]{:S(2)}, u32[]{:S(2)}) collective-permute-start(bf16[384,256]{1,0:T(8,128)(2,1)S(1)} %collective-permute-done.8), channel_id=1, source_target_pairs={{0,4},{4,8},{8,12},{1,5},{5,9},{9,13},{2,6},{6,10},{10,14},{3,7},{... | collective-permute-start | bytes 589832 | tf_op jit(solution)/shard_map/ppermute | solution.py:50
  56.4 11.0 %collective-permute-start.12 = (bf16[384,512]{1,0:T(8,128)(2,1)S(1)}, bf16[384,512]{1,0:T(8,128)(2,1)S(1)}, u32[]{:S(2)}, u32[]{:S(2)}) collective-permute-start(bf16[384,512]{1,0:T(8,128)(2,1)S(1)} %constant_dynamic-update-slice_fusion), channel_id=1, source_target_pairs={{0,1},{1,0},{2,3},{3,2},{4,5},{5,4},{6,7},{7,6},{8,9},{9,8},{10,11... | collective-permute-start | bytes 1179656 | tf_op jit(solution)/shard_map/ppermute | solution.py:39
  59.4 7.0 %collective-permute-start.15 = (bf16[256,640]{0,1:T(8,128)(2,1)S(1)}, bf16[256,640]{0,1:T(8,128)(2,1)S(1)}, u32[]{:S(2)}, u32[]{:S(2)}) collective-permute-start(bf16[256,640]{0,1:T(8,128)(2,1)S(1)} %pad_maximum_fusion.26), channel_id=1, source_target_pairs={{0,1},{1,0},{2,3},{3,2},{4,5},{5,4},{6,7},{7,6},{8,9},{9,8},{10,11... | collective-permute-start | bytes 983048 | tf_op jit(solution)/shard_map/ppermute | solution.py:39
  75.1 6.9 %collective-permute-start.22 = (bf16[640,512]{1,0:T(8,128)(2,1)S(1)}, bf16[640,512]{1,0:T(8,128)(2,1)}, u32[]{:S(2)}, u32[]{:S(2)}) collective-permute-start(bf16[640,512]{1,0:T(8,128)(2,1)S(1)} %get-tuple-element.64), channel_id=1, source_target_pairs={{0,1},{1,0},{2,3},{3,2},{4,5},{5,4},{6,7},{7,6},{8,9},{9,8},{10,11... | collective-permute-start | bytes 1966088 | tf_op jit(solution)/shard_map/ppermute | solution.py:39
  75.6 13.3 %collective-permute-start.17 = (bf16[384,640]{1,0:T(8,128)(2,1)S(1)}, bf16[384,640]{1,0:T(8,128)(2,1)S(1)}, u32[]{:S(2)}, u32[]{:S(2)}) collective-permute-start(bf16[384,640]{1,0:T(8,128)(2,1)S(1)} %fusion.15), channel_id=1, source_target_pairs={{0,2},{1,3},{2,0},{3,1},{4,6},{5,7},{6,4},{7,5},{8,10},{9,11},{10,... | collective-permute-start | bytes 1474568 | tf_op jit(solution)/shard_map/ppermute | solution.py:44
  96.1 12.7 %collective-permute-start.24 = (bf16[384,640]{1,0:T(8,128)(2,1)}, bf16[384,640]{1,0:T(8,128)(2,1)}, u32[]{:S(2)}, u32[]{:S(2)}) collective-permute-start(bf16[384,640]{1,0:T(8,128)(2,1)} %fusion.17), channel_id=1, source_target_pairs={{0,2},{1,3},{2,0},{3,1},{4,6},{5,7},{6,4},{7,5},{8,10},{9,11},{10,... | collective-permute-start | bytes 1474568 | tf_op jit(solution)/shard_map/ppermute | solution.py:44
  121.2 28.7 %collective-permute-start.26 = (bf16[384,640]{1,0:T(8,128)(2,1)S(1)}, bf16[384,640]{1,0:T(8,128)(2,1)S(1)}, u32[]{:S(2)}, u32[]{:S(2)}) collective-permute-start(bf16[384,640]{1,0:T(8,128)(2,1)S(1)} %fusion.16), channel_id=1, source_target_pairs={{0,2},{1,3},{2,0},{3,1},{4,6},{5,7},{6,4},{7,5},{8,10},{9,11},{10,... | collective-permute-start | bytes 1474568 | tf_op jit(solution)/shard_map/ppermute | solution.py:44
  125.2 24.1 %collective-permute-start.27 = (bf16[640,1024]{1,0:T(8,128)(2,1)S(1)}, bf16[640,1024]{1,0:T(8,128)(2,1)S(1)}, u32[]{:S(2)}, u32[]{:S(2)}) collective-permute-start(bf16[640,1024]{1,0:T(8,128)(2,1)S(1)} %fusion), channel_id=1, source_target_pairs={{0,1},{1,0},{2,3},{3,2},{4,5},{5,4},{6,7},{7,6},{8,9},{9,8},{10,11... | collective-permute-start | bytes 3932168 | tf_op jit(solution)/shard_map/ppermute | solution.py:39
  125.5 13.2 %collective-permute-start.25 = (bf16[384,640]{1,0:T(8,128)(2,1)S(1)}, bf16[384,640]{1,0:T(8,128)(2,1)S(1)}, u32[]{:S(2)}, u32[]{:S(2)}) collective-permute-start(bf16[384,640]{1,0:T(8,128)(2,1)S(1)} %get-tuple-element.151), channel_id=1, source_target_pairs={{0,1},{1,0},{2,3},{3,2},{4,5},{5,4},{6,7},{7,6},{8,9},{9,8},{10,11... | collective-permute-start | bytes 1474568 | tf_op jit(solution)/shard_map/ppermute | solution.py:39
  126.1 9.8 %collective-permute-start.29 = (bf16[320,512]{1,0:T(8,128)(2,1)S(1)}, bf16[320,512]{1,0:T(8,128)(2,1)S(1)}, u32[]{:S(2)}, u32[]{:S(2)}) collective-permute-start(bf16[320,512]{1,0:T(8,128)(2,1)S(1)} %reduce-precision_convert_fusion.8), channel_id=1, source_target_pairs={{0,16},{16,0},{1,17},{17,1},{2,18},{18,2},{3,19},{19,3},{4,20},{20... | collective-permute-start | bytes 983048 | tf_op jit(solution)/shard_map/ppermute | solution.py:95
  154.7 10.3 %collective-permute-start.64 = (bf16[160,512]{1,0:T(8,128)(2,1)S(1)}, bf16[160,512]{1,0:T(8,128)(2,1)S(1)}, u32[]{:S(2)}, u32[]{:S(2)}) collective-permute-start(bf16[160,512]{1,0:T(8,128)(2,1)S(1)} %pad_maximum_fusion.37), channel_id=1, source_target_pairs={{0,4},{4,0},{8,12},{12,8},{1,5},{5,1},{9,13},{13,9},{2,6},{6,2},{1... | collective-permute-start | bytes 491528 | tf_op jit(solution)/shard_map/ppermute | solution.py:129
  155.1 13.5 %collective-permute-start.32 = (bf16[320,1024]{1,0:T(8,128)(2,1)S(1)}, bf16[320,1024]{1,0:T(8,128)(2,1)S(1)}, u32[]{:S(2)}, u32[]{:S(2)}) collective-permute-start(bf16[320,1024]{1,0:T(8,128)(2,1)S(1)} %reduce-precision_convert_fusion), channel_id=1, source_target_pairs={{0,16},{16,0},{1,17},{17,1},{2,18},{18,2},{3,19},{19,3},{4,20},{20... | collective-permute-start | bytes 1966088 | tf_op jit(solution)/shard_map/ppermute | solution.py:95
  161.5 20.6 %collective-permute-start.38 = (bf16[768,512]{1,0:T(8,128)(2,1)S(1)}, bf16[768,512]{1,0:T(8,128)(2,1)S(1)}, u32[]{:S(2)}, u32[]{:S(2)}) collective-permute-start(bf16[768,512]{1,0:T(8,128)(2,1)S(1)} %pad_maximum_fusion.13), channel_id=1, source_target_pairs={{0,1},{1,0},{2,3},{3,2},{4,5},{5,4},{6,7},{7,6},{8,9},{9,8},{10,11... | collective-permute-start | bytes 2359304 | tf_op jit(solution)/shard_map/ppermute | solution.py:39
  171.0 8.2 %collective-permute-start.35 = (bf16[160,1024]{1,0:T(8,128)(2,1)S(1)}, bf16[160,1024]{1,0:T(8,128)(2,1)S(1)}, u32[]{:S(2)}, u32[]{:S(2)}) collective-permute-start(bf16[160,1024]{1,0:T(8,128)(2,1)S(1)} %reduce-precision_convert_fusion.7), channel_id=1, source_target_pairs={{0,4},{4,0},{8,12},{12,8},{1,5},{5,1},{9,13},{13,9},{2,6},{6,2},{1... | collective-permute-start | bytes 983048 | tf_op jit(solution)/shard_map/ppermute | solution.py:106
  176.3 12.3 %collective-permute-start.40 = (bf16[640,512]{1,0:T(8,128)(2,1)S(1)}, bf16[640,512]{1,0:T(8,128)(2,1)S(1)}, u32[]{:S(2)}, u32[]{:S(2)}) collective-permute-start(bf16[640,512]{1,0:T(8,128)(2,1)S(1)} %fusion.9), channel_id=1, source_target_pairs={{0,1},{1,0},{2,3},{3,2},{4,5},{5,4},{6,7},{7,6},{8,9},{9,8},{10,11... | collective-permute-start | bytes 1966088 | tf_op jit(solution)/shard_map/ppermute | solution.py:39
  176.6 24.8 %collective-permute-start.34 = (bf16[768,512]{1,0:T(8,128)(2,1)S(1)}, bf16[768,512]{1,0:T(8,128)(2,1)S(1)}, u32[]{:S(2)}, u32[]{:S(2)}) collective-permute-start(bf16[768,512]{1,0:T(8,128)(2,1)S(1)} %pad_maximum_fusion.12), channel_id=1, source_target_pairs={{0,1},{1,0},{2,3},{3,2},{4,5},{5,4},{6,7},{7,6},{8,9},{9,8},{10,11... | collective-permute-start | bytes 2359304 | tf_op jit(solution)/shard_map/ppermute | solution.py:39
  179.3 9.1 %collective-permute-start.36 = (bf16[80,1024]{1,0:T(8,128)(2,1)S(1)}, bf16[80,1024]{1,0:T(8,128)(2,1)S(1)}, u32[]{:S(2)}, u32[]{:S(2)}) collective-permute-start(bf16[80,1024]{1,0:T(8,128)(2,1)S(1)} %reduce-precision_convert_fusion.11), channel_id=1, source_target_pairs={{0,8},{4,12},{8,0},{12,4},{1,9},{5,13},{9,1},{13,5},{2,10},{6,14},... | collective-permute-start | bytes 491528 | tf_op jit(solution)/shard_map/ppermute | solution.py:116
  182.4 16.1 %collective-permute-start.39 = (bf16[2,192,512]{2,1,0:T(8,128)(2,1)S(1)}, bf16[2,192,512]{2,1,0:T(8,128)(2,1)S(1)}, u32[]{:S(2)}, u32[]{:S(2)}) collective-permute-start(bf16[2,192,512]{2,1,0:T(8,128)(2,1)S(1)} %reduce-precision_convert_fusion.3), channel_id=1, source_target_pairs={{0,2},{1,3},{2,0},{3,1},{4,6},{5,7},{6,4},{7,5},{8,10},{9,11},{10,... | collective-permute-start | bytes 1179656 | tf_op jit(solution)/shard_map/ppermute | solution.py:44
  188.5 10.0 %collective-permute-start.46 = (bf16[80,1024]{1,0:T(8,128)(2,1)S(1)}, bf16[80,1024]{1,0:T(8,128)(2,1)S(1)}, u32[]{:S(2)}, u32[]{:S(2)}) collective-permute-start(bf16[80,1024]{1,0:T(8,128)(2,1)S(1)} %reduce-precision_convert_fusion.10), channel_id=1, source_target_pairs={{0,8},{4,12},{8,0},{12,4},{1,9},{5,13},{9,1},{13,5},{2,10},{6,14},... | collective-permute-start | bytes 491528 | tf_op jit(solution)/shard_map/ppermute | solution.py:122
  188.8 12.9 %collective-permute-start.45 = (bf16[320,512]{1,0:T(8,128)(2,1)S(1)}, bf16[320,512]{1,0:T(8,128)(2,1)S(1)}, u32[]{:S(2)}, u32[]{:S(2)}) collective-permute-start(bf16[320,512]{1,0:T(8,128)(2,1)S(1)} %reduce-precision_convert_fusion.6), channel_id=1, source_target_pairs={{0,16},{16,0},{1,17},{17,1},{2,18},{18,2},{3,19},{19,3},{4,20},{20... | collective-permute-start | bytes 983048 | tf_op jit(solution)/shard_map/ppermute | solution.py:95
  198.5 16.1 %collective-permute-start.63 = (bf16[160,1024]{1,0:T(8,128)(2,1)S(1)}, bf16[160,1024]{1,0:T(8,128)(2,1)S(1)}, u32[]{:S(2)}, u32[]{:S(2)}) collective-permute-start(bf16[160,1024]{1,0:T(8,128)(2,1)S(1)} %pad_maximum_fusion.27), channel_id=1, source_target_pairs={{0,4},{4,0},{8,12},{12,8},{1,5},{5,1},{9,13},{13,9},{2,6},{6,2},{1... | collective-permute-start | bytes 983048 | tf_op jit(solution)/shard_map/ppermute | solution.py:129
  198.8 16.2 %collective-permute-start.41 = (bf16[192,512]{1,0:T(8,128)(2,1)S(1)}, bf16[192,512]{1,0:T(8,128)(2,1)S(1)}, u32[]{:S(2)}, u32[]{:S(2)}) collective-permute-start(bf16[192,512]{1,0:T(8,128)(2,1)S(1)} %get-tuple-element.159), channel_id=1, source_target_pairs={{12,0},{13,1},{14,2},{15,3},{28,16},{29,17},{30,18},{31,19}} | collective-permute-start | bytes 589832 | tf_op jit(solution)/shard_map/ppermute | solution.py:50
  200.1 18.2 %collective-permute-start.43 = (bf16[192,512]{1,0:T(8,128)(2,1)S(1)}, bf16[192,512]{1,0:T(8,128)(2,1)S(1)}, u32[]{:S(2)}, u32[]{:S(2)}) collective-permute-start(bf16[192,512]{1,0:T(8,128)(2,1)S(1)} %get-tuple-element.158), channel_id=1, source_target_pairs={{8,0},{12,4},{9,1},{13,5},{10,2},{14,6},{11,3},{15,7},{24,16},{28,... | collective-permute-start | bytes 589832 | tf_op jit(solution)/shard_map/ppermute | solution.py:50
  201.7 13.3 %collective-permute-start.37 = (bf16[2,192,512]{2,1,0:T(8,128)(2,1)S(1)}, bf16[2,192,512]{2,1,0:T(8,128)(2,1)S(1)}, u32[]{:S(2)}, u32[]{:S(2)}) collective-permute-start(bf16[2,192,512]{2,1,0:T(8,128)(2,1)S(1)} %reduce-precision_convert_fusion.4), channel_id=1, source_target_pairs={{0,2},{1,3},{2,0},{3,1},{4,6},{5,7},{6,4},{7,5},{8,10},{9,11},{10,... | collective-permute-start | bytes 1179656 | tf_op jit(solution)/shard_map/ppermute | solution.py:44
  215.1 7.9 %collective-permute-start.44 = (bf16[192,512]{1,0:T(8,128)(2,1)S(1)}, bf16[192,512]{1,0:T(8,128)(2,1)S(1)}, u32[]{:S(2)}, u32[]{:S(2)}) collective-permute-start(bf16[192,512]{1,0:T(8,128)(2,1)S(1)} %fusion.69), channel_id=1, source_target_pairs={{4,0},{8,4},{12,8},{5,1},{9,5},{13,9},{6,2},{10,6},{14,10},{7,3},{... | collective-permute-start | bytes 589832 | tf_op jit(solution)/shard_map/ppermute | solution.py:50
  216.8 17.6 %collective-permute-start.42 = (bf16[384,640]{1,0:T(8,128)(2,1)S(1)}, bf16[384,640]{1,0:T(8,128)(2,1)S(1)}, u32[]{:S(2)}, u32[]{:S(2)}) collective-permute-start(bf16[384,640]{1,0:T(8,128)(2,1)S(1)} %reduce-precision_convert_fusion.1), channel_id=1, source_target_pairs={{0,2},{1,3},{2,0},{3,1},{4,6},{5,7},{6,4},{7,5},{8,10},{9,11},{10,... | collective-permute-start | bytes 1474568 | tf_op jit(solution)/shard_map/ppermute | solution.py:44
  226.1 8.3 %collective-permute-start.47 = (bf16[192,640]{1,0:T(8,128)(2,1)S(1)}, bf16[192,640]{1,0:T(8,128)(2,1)S(1)}, u32[]{:S(2)}, u32[]{:S(2)}) collective-permute-start(bf16[192,640]{1,0:T(8,128)(2,1)S(1)} %get-tuple-element.81), channel_id=1, source_target_pairs={{0,2},{1,3},{2,0},{3,1},{4,6},{5,7},{6,4},{7,5},{8,10},{9,11},{10,... | collective-permute-start | bytes 737288 | tf_op jit(solution)/shard_map/ppermute | solution.py:44
  227.6 7.8 %collective-permute-start.49 = (bf16[672,256]{1,0:T(8,128)(2,1)S(1)}, bf16[672,256]{1,0:T(8,128)(2,1)S(1)}, u32[]{:S(2)}, u32[]{:S(2)}) collective-permute-start(bf16[672,256]{1,0:T(8,128)(2,1)S(1)} %reduce-precision_convert_fusion.5), channel_id=1, source_target_pairs={{0,1},{1,0},{2,3},{3,2},{4,5},{5,4},{6,7},{7,6},{8,9},{9,8},{10,11... | collective-permute-start | bytes 1032200 | tf_op jit(solution)/shard_map/ppermute | solution.py:39
  235.3 29.3 %collective-permute-start.48 = (f32[384,640]{1,0:T(8,128)S(1)}, f32[384,640]{1,0:T(8,128)S(1)}, u32[]{:S(2)}, u32[]{:S(2)}) collective-permute-start(f32[384,640]{1,0:T(8,128)S(1)} %multiply_add_fusion), channel_id=1, source_target_pairs={{0,1},{1,0},{2,3},{3,2},{4,5},{5,4},{6,7},{7,6},{8,9},{9,8},{10,11... | collective-permute-start | bytes 2949128 | tf_op jit(solution)/shard_map/ppermute | solution.py:39
  241.4 8.9 %collective-permute-start.61 = (bf16[80,512]{1,0:T(8,128)(2,1)S(1)}, bf16[80,512]{1,0:T(8,128)(2,1)S(1)}, u32[]{:S(2)}, u32[]{:S(2)}) collective-permute-start(bf16[80,512]{1,0:T(8,128)(2,1)S(1)} %reduce-precision_convert_fusion.18), channel_id=1, source_target_pairs={{0,8},{4,12},{8,0},{12,4},{1,9},{5,13},{9,1},{13,5},{2,10},{6,14},... | collective-permute-start | bytes 245768 | tf_op jit(solution)/shard_map/ppermute | solution.py:122
  244.8 9.6 %collective-permute-start.55 = (bf16[336,128]{1,0:T(8,128)(2,1)S(1)}, bf16[336,128]{1,0:T(8,128)(2,1)S(1)}, u32[]{:S(2)}, u32[]{:S(2)}) collective-permute-start(bf16[336,128]{1,0:T(8,128)(2,1)S(1)} %reduce-precision_convert_fusion.14), channel_id=1, source_target_pairs={{0,8},{4,12},{8,0},{12,4},{1,9},{5,13},{9,1},{13,5},{2,10},{6,14},... | collective-permute-start | bytes 258056 | tf_op jit(solution)/shard_map/ppermute | solution.py:138
  246.5 8.0 %collective-permute-start.56 = (bf16[336,128]{1,0:T(8,128)(2,1)S(1)}, bf16[336,128]{1,0:T(8,128)(2,1)S(1)}, u32[]{:S(2)}, u32[]{:S(2)}) collective-permute-start(bf16[336,128]{1,0:T(8,128)(2,1)S(1)} %reduce-precision_convert_fusion.14), channel_id=1, source_target_pairs={{0,4},{4,8},{8,12},{12,0},{1,5},{5,9},{9,13},{13,1},{2,6},{6,10},{... | collective-permute-start | bytes 258056 | tf_op jit(solution)/shard_map/ppermute | solution.py:138
  255.5 8.1 %collective-permute-start.62 = (bf16[160,512]{1,0:T(8,128)(2,1)S(1)}, bf16[160,512]{1,0:T(8,128)(2,1)S(1)}, u32[]{:S(2)}, u32[]{:S(2)}) collective-permute-start(bf16[160,512]{1,0:T(8,128)(2,1)S(1)} %pad_maximum_fusion.38), channel_id=1, source_target_pairs={{0,4},{4,0},{8,12},{12,8},{1,5},{5,1},{9,13},{13,9},{2,6},{6,2},{1... | collective-permute-start | bytes 491528 | tf_op jit(solution)/shard_map/ppermute | solution.py:129
  (103 other events, 606.4 us)
where the time goes:
time: 271 us; the launch traced here: 266 us
  waiting for transfers between devices  109 us (40%)
  starting transfers between devices  71.9 us (27%)
  other arithmetic  30.4 us (11%)
  matrix products  27.8 us (10%)
  local copies, waits for them, and re-layouts  24.4 us (9%)
  between operations  3.4 us (1%)
    ppermute x9, starting transfers between devices, over_context(): return lax.ppermute(array, 'context', pairs)  24.6 us
    ppermute x8, waiting for transfers between devices, over_pairs(): return lax.ppermute(array, 'tensor', [(i, i ^ 2) for i in range(devices)])  20 us
    unnamed x182, local copies, waits for them, and re-layouts  16.5 us
    ppermute x9, waiting for transfers between devices, over_context(): return lax.ppermute(array, 'context', pairs)  15.6 us
    ppermute x8, waiting for transfers between devices, dp_gathered(): other = lax.ppermute(array, 'dp', [(0, 1), (1, 0)])  14.1 us
    ppermute x3, waiting for transfers between devices, spread_near(): other = lax.ppermute(part, 'context', [(i, i ^ 1) for i in range(4)])  12.8 us
    ppermute x3, waiting for transfers between devices, dp_scattered(): lax.ppermute(low(send), 'dp', [(0, 1), (1, 0)]).astype(F32)  12.4 us
    dot_general x13, matrix products, product_rt(): lax.dot_general(left_side, right_side, (((1,), (1,)), ((), ())), preferre...  9.9 us
  transfers between devices with their start and end apart: 65, of which 28 were waited for; matrix products, arithmetic and copies ran while one was open for 18% of the time, Pallas kernels for 0%

commit v1 on v0

--- a/solution.py
+++ b/solution.py
@@ -233,7 +233,9 @@
     w_key = dp_gathered(key_weight)
     w_value = dp_gathered(value_weight)
     gain_parts = dp_gathered(gains).reshape(dp_count, 16, shard + head_shard)
-    query_weight, output_weight = after((query_weight, output_weight), (w_key, w_value))
+    w_key, w_value, query_weight, output_weight = lax.optimization_barrier(
+        (w_key, w_value, query_weight, output_weight)
+    )
     w_query = dp_gathered(query_weight)
     w_out = dp_gathered(output_weight, axis=1)
     gate_weight, up_weight, down_weight = after(
@@ -506,7 +508,7 @@
     small = owners_sum(small, columns // 2)
     other = over_pairs(grad_normed_kv)
     grad_normed = grad_normed + ordered(pair, grad_normed_kv, other).astype(F32)
-    tokens_own = grad_middle + norm_back(grad_normed, g_input, input_unit, input_inverse)
+    tokens_own = low(grad_middle + norm_back(grad_normed, g_input, input_unit, input_inverse))
     tokens_other = over_core(tokens_own)
     small = after(small, far_qo)
     total_gate_up = spread_near(all_gate_up)
@@ -514,7 +516,7 @@
     small = low(context_sum_small(small))
     total_qo = spread_near(all_qo)
     total_down = spread_near(all_down)
-    tokens_grad = ordered(core, tokens_own, tokens_other)
+    tokens_grad = ordered(core, tokens_own, tokens_other).astype(F32)
     over_both = partner(small, 0, 3)
     other_core = over_core(small)
     small = ordered(pair, small, over_pairs(small), axis=1)

time: 271 us -> 267 us (0.985)
  waiting for transfers between devices: 109 us -> 94.8 us
  starting transfers between devices: 71.9 us -> 81.2 us
    ppermute x8, waiting for transfers between devices: 14.1 us -> 2.99 us  [dp_gathered(): other = lax.ppermute(array, 'dp', [(0, 1), (1, 0)])]
    ppermute x8, starting transfers between devices: 6.46 us -> 9.6 us  [over_pairs(): return lax.ppermute(array, 'tensor', [(i, i ^ 2) for i in range(devices)])]
    ppermute x9, starting transfers between devices: 24.6 us -> 27.4 us  [over_context(): return lax.ppermute(array, 'context', pairs)]
    unnamed x182 -> x171, local copies, waits for them, and re-layouts: 16.5 us -> 16.4 us
where the time goes in v1:
time: 267 us; the launch traced here: 262 us
  waiting for transfers between devices  94.8 us (36%)
  starting transfers between devices  81.2 us (30%)
  other arithmetic  30.4 us (11%)
  matrix products  27.7 us (10%)
  local copies, waits for them, and re-layouts  24.4 us (9%)
  between operations  3.32 us (1%)
    ppermute x9, starting transfers between devices, over_context(): return lax.ppermute(array, 'context', pairs)  27.4 us
    ppermute x8, waiting for transfers between devices, over_pairs(): return lax.ppermute(array, 'tensor', [(i, i ^ 2) for i in range(devices)])  20 us
    unnamed x171, local copies, waits for them, and re-layouts  16.4 us
    ppermute x9, waiting for transfers between devices, over_context(): return lax.ppermute(array, 'context', pairs)  15 us
    ppermute x3, waiting for transfers between devices, spread_near(): other = lax.ppermute(part, 'context', [(i, i ^ 1) for i in range(4)])  12.9 us
    ppermute x8, starting transfers between devices, dp_gathered(): other = lax.ppermute(array, 'dp', [(0, 1), (1, 0)])  10.6 us
    ppermute x3, waiting for transfers between devices, dp_scattered(): lax.ppermute(low(send), 'dp', [(0, 1), (1, 0)]).astype(F32)  9.92 us
    dot_general x13, matrix products, product_rt(): lax.dot_general(left_side, right_side, (((1,), (1,)), ((), ())), preferre...  9.89 us
  transfers between devices with their start and end apart: 65, of which 28 were waited for; matrix products, arithmetic and copies ran while one was open for 18% of the time, Pallas kernels for 0%

profile of v1, /device:TPU:0, one launch (start us, length us, event | category | flops | bytes accessed | tf_op | source)
XLA Modules:
  0.0 261.7 jit_solution(8456286231261201299)
XLA Ops:
  0.7 3.0 %collective-permute-start.1 = (bf16[320,256]{1,0:T(8,128)(2,1)}, bf16[320,256]{1,0:T(8,128)(2,1)S(1)}, u32[]{:S(2)}, u32[]{:S(2)}) collective-permute-start(bf16[320,256]{1,0:T(8,128)(2,1)} %param.20), channel_id=1, source_target_pairs={{0,16},{16,0},{1,17},{17,1},{2,18},{18,2},{3,19},{19,3},{4,20},{20... | collective-permute-start | bytes 491528 | tf_op jit(solution)/shard_map/ppermute | solution.py:84
  5.5 2.0 collective-permute-start
  10.3 1.6 collective-permute-done
  13.8 1.7 collective-permute-start.4
  15.9 3.7 %collective-permute-start.7 = (bf16[384,256]{1,0:T(8,128)(2,1)S(1)}, bf16[384,256]{1,0:T(8,128)(2,1)S(1)}, u32[]{:S(2)}, u32[]{:S(2)}) collective-permute-start(bf16[384,256]{1,0:T(8,128)(2,1)S(1)} %slice.600), channel_id=1, source_target_pairs={{0,4},{4,8},{8,12},{1,5},{5,9},{9,13},{2,6},{6,10},{10,14},{3,7},{... | collective-permute-start | bytes 589832 | tf_op jit(solution)/shard_map/ppermute | solution.py:50
  20.8 3.6 %collective-permute-start.5 = (bf16[384,256]{1,0:T(8,128)(2,1)S(1)}, bf16[384,256]{1,0:T(8,128)(2,1)S(1)}, u32[]{:S(2)}, u32[]{:S(2)}) collective-permute-start(bf16[384,256]{1,0:T(8,128)(2,1)S(1)} %pad_maximum_fusion.33), channel_id=1, source_target_pairs={{0,4},{4,8},{8,12},{1,5},{5,9},{9,13},{2,6},{6,10},{10,14},{3,7},{... | collective-permute-start | bytes 589832 | tf_op jit(solution)/shard_map/ppermute | solution.py:50
  24.6 1.6 collective-permute-start.20
  26.7 2.5 collective-permute-done.5
  29.2 4.4 %collective-permute-start.6 = (bf16[384,256]{1,0:T(8,128)(2,1)S(1)}, bf16[384,256]{1,0:T(8,128)(2,1)S(1)}, u32[]{:S(2)}, u32[]{:S(2)}) collective-permute-start(bf16[384,256]{1,0:T(8,128)(2,1)S(1)} %collective-permute-done.5), channel_id=1, source_target_pairs={{0,4},{4,8},{8,12},{1,5},{5,9},{9,13},{2,6},{6,10},{10,14},{3,7},{... | collective-permute-start | bytes 589832 | tf_op jit(solution)/shard_map/ppermute | solution.py:50
  33.6 3.5 %collective-permute-start.8 = (bf16[384,256]{1,0:T(8,128)(2,1)S(1)}, bf16[384,256]{1,0:T(8,128)(2,1)S(1)}, u32[]{:S(2)}, u32[]{:S(2)}) collective-permute-start(bf16[384,256]{1,0:T(8,128)(2,1)S(1)} %collective-permute-done.7), channel_id=1, source_target_pairs={{0,4},{4,8},{8,12},{1,5},{5,9},{9,13},{2,6},{6,10},{10,14},{3,7},{... | collective-permute-start | bytes 589832 | tf_op jit(solution)/shard_map/ppermute | solution.py:50
  40.0 1.8 collective-permute-done.8
  42.7 4.4 %collective-permute-start.13 = (bf16[384,256]{1,0:T(8,128)(2,1)S(1)}, bf16[384,256]{1,0:T(8,128)(2,1)S(1)}, u32[]{:S(2)}, u32[]{:S(2)}) collective-permute-start(bf16[384,256]{1,0:T(8,128)(2,1)S(1)} %collective-permute-done.6), channel_id=1, source_target_pairs={{0,4},{4,8},{8,12},{1,5},{5,9},{9,13},{2,6},{6,10},{10,14},{3,7},{... | collective-permute-start | bytes 589832 | tf_op jit(solution)/shard_map/ppermute | solution.py:50
  48.5 3.6 %collective-permute-start.14 = (bf16[384,256]{1,0:T(8,128)(2,1)S(1)}, bf16[384,256]{1,0:T(8,128)(2,1)S(1)}, u32[]{:S(2)}, u32[]{:S(2)}) collective-permute-start(bf16[384,256]{1,0:T(8,128)(2,1)S(1)} %collective-permute-done.8), channel_id=1, source_target_pairs={{0,4},{4,8},{8,12},{1,5},{5,9},{9,13},{2,6},{6,10},{10,14},{3,7},{... | collective-permute-start | bytes 589832 | tf_op jit(solution)/shard_map/ppermute | solution.py:50
  52.3 3.8 %collective-permute-done.14 = bf16[384,256]{1,0:T(8,128)(2,1)S(1)} collective-permute-done((bf16[384,256]{1,0:T(8,128)(2,1)S(1)}, bf16[384,256]{1,0:T(8,128)(2,1)S(1)}, u32[]{:S(2)}, u32[]{:S(2)}) %collective-permute-start.14) | collective-permute-done | bytes 196640 | tf_op jit(solution)/shard_map/ppermute | solution.py:50
  68.5 1.6 collective-permute-start.17
  74.9 1.6 constant_dynamic-update-slice_fusion.16
  76.6 5.2 %collective-permute-done.17 = bf16[384,640]{1,0:T(8,128)(2,1)S(1)} collective-permute-done((bf16[384,640]{1,0:T(8,128)(2,1)S(1)}, bf16[384,640]{1,0:T(8,128)(2,1)S(1)}, u32[]{:S(2)}, u32[]{:S(2)}) %collective-permute-start.17) | collective-permute-done | bytes 491552 | tf_op jit(solution)/shard_map/ppermute | solution.py:44
  87.4 1.6 fusion.17
  90.7 11.1 %collective-permute-done.24 = bf16[384,640]{1,0:T(8,128)(2,1)} collective-permute-done((bf16[384,640]{1,0:T(8,128)(2,1)}, bf16[384,640]{1,0:T(8,128)(2,1)}, u32[]{:S(2)}, u32[]{:S(2)}) %collective-permute-start.24) | collective-permute-done | bytes 491552 | tf_op jit(solution)/shard_map/ppermute | solution.py:44
  103.1 1.9 fusion.25
  105.1 2.0 fusion.23
  108.9 1.7 fusion.7
  110.8 1.6 copy-done.22
  114.0 1.6 collective-permute-start.26
  115.6 1.6 fusion.115
  119.0 1.5 collective-permute-start.29
  120.7 8.2 %collective-permute-done.29 = bf16[320,512]{1,0:T(8,128)(2,1)S(1)} collective-permute-done((bf16[320,512]{1,0:T(8,128)(2,1)S(1)}, bf16[320,512]{1,0:T(8,128)(2,1)S(1)}, u32[]{:S(2)}, u32[]{:S(2)}) %collective-permute-start.29) | collective-permute-done | bytes 327712 | tf_op jit(solution)/shard_map/ppermute | solution.py:95
  129.0 2.5 collective-permute-start.30
  131.6 3.6 %collective-permute-done.30 = bf16[160,512]{1,0:T(8,128)(2,1)S(1)} collective-permute-done((bf16[160,512]{1,0:T(8,128)(2,1)S(1)}, bf16[160,512]{1,0:T(8,128)(2,1)S(1)}, u32[]{:S(2)}, u32[]{:S(2)}) %collective-permute-start.30) | collective-permute-done | bytes 163872 | tf_op jit(solution)/shard_map/ppermute | solution.py:106
  135.3 2.8 %collective-permute-start.31 = (bf16[80,512]{1,0:T(8,128)(2,1)S(1)}, bf16[80,512]{1,0:T(8,128)(2,1)S(1)}, u32[]{:S(2)}, u32[]{:S(2)}) collective-permute-start(bf16[80,512]{1,0:T(8,128)(2,1)S(1)} %reduce-precision_convert_fusion.22), channel_id=1, source_target_pairs={{0,8},{4,12},{8,0},{12,4},{1,9},{5,13},{9,1},{13,5},{2,10},{6,14},... | collective-permute-start | bytes 245768 | tf_op jit(solution)/shard_map/ppermute | solution.py:116
  139.2 1.5 collective-permute-done.31
  140.7 2.8 %collective-permute-start.33 = (bf16[80,512]{1,0:T(8,128)(2,1)S(1)}, bf16[80,512]{1,0:T(8,128)(2,1)S(1)}, u32[]{:S(2)}, u32[]{:S(2)}) collective-permute-start(bf16[80,512]{1,0:T(8,128)(2,1)S(1)} %reduce-precision_convert_fusion.21), channel_id=1, source_target_pairs={{0,8},{4,12},{8,0},{12,4},{1,9},{5,13},{9,1},{13,5},{2,10},{6,14},... | collective-permute-start | bytes 245768 | tf_op jit(solution)/shard_map/ppermute | solution.py:122
  161.0 1.7 collective-permute-done.32
  165.1 1.6 collective-permute-start.35
  172.4 1.9 collective-permute-done.35
  176.8 6.8 %collective-permute-done.36 = bf16[80,1024]{1,0:T(8,128)(2,1)S(1)} collective-permute-done((bf16[80,1024]{1,0:T(8,128)(2,1)S(1)}, bf16[80,1024]{1,0:T(8,128)(2,1)S(1)}, u32[]{:S(2)}, u32[]{:S(2)}) %collective-permute-start.36) | collective-permute-done | bytes 163872 | tf_op jit(solution)/shard_map/ppermute | solution.py:116
  184.6 7.2 %collective-permute-done.46 = bf16[80,1024]{1,0:T(8,128)(2,1)S(1)} collective-permute-done((bf16[80,1024]{1,0:T(8,128)(2,1)S(1)}, bf16[80,1024]{1,0:T(8,128)(2,1)S(1)}, u32[]{:S(2)}, u32[]{:S(2)}) %collective-permute-start.46) | collective-permute-done | bytes 163872 | tf_op jit(solution)/shard_map/ppermute | solution.py:122
  196.5 12.9 %collective-permute-done.63 = bf16[160,1024]{1,0:T(8,128)(2,1)S(1)} collective-permute-done((bf16[160,1024]{1,0:T(8,128)(2,1)S(1)}, bf16[160,1024]{1,0:T(8,128)(2,1)S(1)}, u32[]{:S(2)}, u32[]{:S(2)}) %collective-permute-start.63) | collective-permute-done | bytes 327712 | tf_op jit(solution)/shard_map/ppermute | solution.py:129
  210.0 1.6 collective-permute-start.44
  212.6 5.4 %collective-permute-done.44 = bf16[192,512]{1,0:T(8,128)(2,1)S(1)} collective-permute-done((bf16[192,512]{1,0:T(8,128)(2,1)S(1)}, bf16[192,512]{1,0:T(8,128)(2,1)S(1)}, u32[]{:S(2)}, u32[]{:S(2)}) %collective-permute-start.44) | collective-permute-done | bytes 196640 | tf_op jit(solution)/shard_map/ppermute | solution.py:50
  223.0 3.2 %collective-permute-done.53 = bf16[160,512]{1,0:T(8,128)(2,1)S(1)} collective-permute-done((bf16[160,512]{1,0:T(8,128)(2,1)S(1)}, bf16[160,512]{1,0:T(8,128)(2,1)S(1)}, u32[]{:S(2)}, u32[]{:S(2)}) %collective-permute-start.53) | collective-permute-done | bytes 163872 | tf_op jit(solution)/shard_map/ppermute | solution.py:106
  226.2 3.0 %collective-permute-done.47 = bf16[192,640]{1,0:T(8,128)(2,1)S(1)} collective-permute-done((bf16[192,640]{1,0:T(8,128)(2,1)S(1)}, bf16[192,640]{1,0:T(8,128)(2,1)S(1)}, u32[]{:S(2)}, u32[]{:S(2)}) %collective-permute-start.47) | collective-permute-done | bytes 245792 | tf_op jit(solution)/shard_map/ppermute | solution.py:44
  233.1 2.4 collective-permute-start.52
  239.7 1.6 collective-permute-start.55
  241.4 2.4 collective-permute-start.56
  245.9 3.3 %collective-permute-done.55 = bf16[336,128]{1,0:T(8,128)(2,1)S(1)} collective-permute-done((bf16[336,128]{1,0:T(8,128)(2,1)S(1)}, bf16[336,128]{1,0:T(8,128)(2,1)S(1)}, u32[]{:S(2)}, u32[]{:S(2)}) %collective-permute-start.55) | collective-permute-done | bytes 86048 | tf_op jit(solution)/shard_map/ppermute | solution.py:138
  251.0 1.5 collective-permute-start.62
  254.6 2.2 collective-permute-done.60
  (486 shorter events, 103.9 us)
Async XLA Ops:
  0.7 12.0 %collective-permute-start.1 = (bf16[320,256]{1,0:T(8,128)(2,1)}, bf16[320,256]{1,0:T(8,128)(2,1)S(1)}, u32[]{:S(2)}, u32[]{:S(2)}) collective-permute-start(bf16[320,256]{1,0:T(8,128)(2,1)} %param.20), channel_id=1, source_target_pairs={{0,16},{16,0},{1,17},{17,1},{2,18},{18,2},{3,19},{19,3},{4,20},{20... | collective-permute-start | bytes 491528 | tf_op jit(solution)/shard_map/ppermute | solution.py:84
  3.7 9.0 %collective-permute-start.2 = (bf16[320,256]{1,0:T(8,128)(2,1)}, bf16[320,256]{1,0:T(8,128)(2,1)S(1)}, u32[]{:S(2)}, u32[]{:S(2)}) collective-permute-start(bf16[320,256]{1,0:T(8,128)(2,1)} %param.21), channel_id=1, source_target_pairs={{0,16},{16,0},{1,17},{17,1},{2,18},{18,2},{3,19},{19,3},{4,20},{20... | collective-permute-start | bytes 491528 | tf_op jit(solution)/shard_map/ppermute | solution.py:84
  13.8 10.6 %collective-permute-start.4 = (bf16[256,320]{0,1:T(8,128)(2,1)S(1)}, bf16[256,320]{0,1:T(8,128)(2,1)S(1)}, u32[]{:S(2)}, u32[]{:S(2)}) collective-permute-start(bf16[256,320]{0,1:T(8,128)(2,1)S(1)} %copy-done.69), channel_id=1, source_target_pairs={{0,16},{16,0},{1,17},{17,1},{2,18},{18,2},{3,19},{19,3},{4,20},{20... | collective-permute-start | bytes 491528 | tf_op jit(solution)/shard_map/ppermute | solution.py:84
  15.6 8.9 %collective-permute-start.3 = (bf16[320,256]{1,0:T(8,128)(2,1)S(1)}, bf16[320,256]{1,0:T(8,128)(2,1)S(1)}, u32[]{:S(2)}, u32[]{:S(2)}) collective-permute-start(bf16[320,256]{1,0:T(8,128)(2,1)S(1)} %copy-done.70), channel_id=1, source_target_pairs={{0,16},{16,0},{1,17},{17,1},{2,18},{18,2},{3,19},{19,3},{4,20},{20... | collective-permute-start | bytes 491528 | tf_op jit(solution)/shard_map/ppermute | solution.py:84
  15.9 17.7 %collective-permute-start.7 = (bf16[384,256]{1,0:T(8,128)(2,1)S(1)}, bf16[384,256]{1,0:T(8,128)(2,1)S(1)}, u32[]{:S(2)}, u32[]{:S(2)}) collective-permute-start(bf16[384,256]{1,0:T(8,128)(2,1)S(1)} %slice.600), channel_id=1, source_target_pairs={{0,4},{4,8},{8,12},{1,5},{5,9},{9,13},{2,6},{6,10},{10,14},{3,7},{... | collective-permute-start | bytes 589832 | tf_op jit(solution)/shard_map/ppermute | solution.py:50
  20.7 21.2 %collective-permute-start.10 = (bf16[384,512]{1,0:T(8,128)(2,1)S(1)}, bf16[384,512]{1,0:T(8,128)(2,1)S(1)}, u32[]{:S(2)}, u32[]{:S(2)}) collective-permute-start(bf16[384,512]{1,0:T(8,128)(2,1)S(1)} %pad_maximum_fusion.20), channel_id=1, source_target_pairs={{0,1},{1,0},{2,3},{3,2},{4,5},{5,4},{6,7},{7,6},{8,9},{9,8},{10,11... | collective-permute-start | bytes 1179656 | tf_op jit(solution)/shard_map/ppermute | solution.py:39
  20.8 8.4 %collective-permute-start.5 = (bf16[384,256]{1,0:T(8,128)(2,1)S(1)}, bf16[384,256]{1,0:T(8,128)(2,1)S(1)}, u32[]{:S(2)}, u32[]{:S(2)}) collective-permute-start(bf16[384,256]{1,0:T(8,128)(2,1)S(1)} %pad_maximum_fusion.33), channel_id=1, source_target_pairs={{0,4},{4,8},{8,12},{1,5},{5,9},{9,13},{2,6},{6,10},{10,14},{3,7},{... | collective-permute-start | bytes 589832 | tf_op jit(solution)/shard_map/ppermute | solution.py:50
  24.6 18.0 %collective-permute-start.20 = (bf16[320,512]{1,0:T(8,128)(2,1)S(1)}, bf16[320,512]{1,0:T(8,128)(2,1)S(1)}, u32[]{:S(2)}, u32[]{:S(2)}) collective-permute-start(bf16[320,512]{1,0:T(8,128)(2,1)S(1)} %bitcast.90), channel_id=1, source_target_pairs={{0,16},{16,0},{1,17},{17,1},{2,18},{18,2},{3,19},{19,3},{4,20},{20... | collective-permute-start | bytes 983048 | tf_op jit(solution)/shard_map/ppermute | solution.py:84
  26.1 16.6 %collective-permute-start.19 = (bf16[320,512]{1,0:T(8,128)(2,1)S(1)}, bf16[320,512]{1,0:T(8,128)(2,1)S(1)}, u32[]{:S(2)}, u32[]{:S(2)}) collective-permute-start(bf16[320,512]{1,0:T(8,128)(2,1)S(1)} %copy-done.61), channel_id=1, source_target_pairs={{0,16},{16,0},{1,17},{17,1},{2,18},{18,2},{3,19},{19,3},{4,20},{20... | collective-permute-start | bytes 983048 | tf_op jit(solution)/shard_map/ppermute | solution.py:84
  29.2 9.3 %collective-permute-start.6 = (bf16[384,256]{1,0:T(8,128)(2,1)S(1)}, bf16[384,256]{1,0:T(8,128)(2,1)S(1)}, u32[]{:S(2)}, u32[]{:S(2)}) collective-permute-start(bf16[384,256]{1,0:T(8,128)(2,1)S(1)} %collective-permute-done.5), channel_id=1, source_target_pairs={{0,4},{4,8},{8,12},{1,5},{5,9},{9,13},{2,6},{6,10},{10,14},{3,7},{... | collective-permute-start | bytes 589832 | tf_op jit(solution)/shard_map/ppermute | solution.py:50
  33.6 8.2 %collective-permute-start.8 = (bf16[384,256]{1,0:T(8,128)(2,1)S(1)}, bf16[384,256]{1,0:T(8,128)(2,1)S(1)}, u32[]{:S(2)}, u32[]{:S(2)}) collective-permute-start(bf16[384,256]{1,0:T(8,128)(2,1)S(1)} %collective-permute-done.7), channel_id=1, source_target_pairs={{0,4},{4,8},{8,12},{1,5},{5,9},{9,13},{2,6},{6,10},{10,14},{3,7},{... | collective-permute-start | bytes 589832 | tf_op jit(solution)/shard_map/ppermute | solution.py:50
  38.5 10.0 %collective-permute-start.18 = (bf16[320,512]{1,0:T(8,128)(2,1)S(1)}, bf16[320,512]{1,0:T(8,128)(2,1)S(1)}, u32[]{:S(2)}, u32[]{:S(2)}) collective-permute-start(bf16[320,512]{1,0:T(8,128)(2,1)S(1)} %copy-done.62), channel_id=1, source_target_pairs={{0,16},{16,0},{1,17},{17,1},{2,18},{18,2},{3,19},{19,3},{4,20},{20... | collective-permute-start | bytes 983048 | tf_op jit(solution)/shard_map/ppermute | solution.py:84
  41.8 16.1 %collective-permute-start.11 = (bf16[384,512]{1,0:T(8,128)(2,1)S(1)}, bf16[384,512]{1,0:T(8,128)(2,1)S(1)}, u32[]{:S(2)}, u32[]{:S(2)}) collective-permute-start(bf16[384,512]{1,0:T(8,128)(2,1)S(1)} %constant_dynamic-update-slice_fusion.10), channel_id=1, source_target_pairs={{0,1},{1,0},{2,3},{3,2},{4,5},{5,4},{6,7},{7,6},{8,9},{9,8},{10,11... | collective-permute-start | bytes 1179656 | tf_op jit(solution)/shard_map/ppermute | solution.py:39
  41.9 14.3 %collective-permute-start.9 = (bf16[640,256]{1,0:T(8,128)(2,1)S(1)}, bf16[640,256]{1,0:T(8,128)(2,1)S(1)}, u32[]{:S(2)}, u32[]{:S(2)}) collective-permute-start(bf16[640,256]{1,0:T(8,128)(2,1)S(1)} %pad_maximum_fusion.26), channel_id=1, source_target_pairs={{0,1},{1,0},{2,3},{3,2},{4,5},{5,4},{6,7},{7,6},{8,9},{9,8},{10,11... | collective-permute-start | bytes 983048 | tf_op jit(solution)/shard_map/ppermute | solution.py:39
  42.6 17.7 %collective-permute-start.12 = (bf16[384,512]{1,0:T(8,128)(2,1)S(1)}, bf16[384,512]{1,0:T(8,128)(2,1)S(1)}, u32[]{:S(2)}, u32[]{:S(2)}) collective-permute-start(bf16[384,512]{1,0:T(8,128)(2,1)S(1)} %constant_dynamic-update-slice_fusion.2), channel_id=1, source_target_pairs={{0,1},{1,0},{2,3},{3,2},{4,5},{5,4},{6,7},{7,6},{8,9},{9,8},{10,11... | collective-permute-start | bytes 1179656 | tf_op jit(solution)/shard_map/ppermute | solution.py:39
  42.7 9.6 %collective-permute-start.13 = (bf16[384,256]{1,0:T(8,128)(2,1)S(1)}, bf16[384,256]{1,0:T(8,128)(2,1)S(1)}, u32[]{:S(2)}, u32[]{:S(2)}) collective-permute-start(bf16[384,256]{1,0:T(8,128)(2,1)S(1)} %collective-permute-done.6), channel_id=1, source_target_pairs={{0,4},{4,8},{8,12},{1,5},{5,9},{9,13},{2,6},{6,10},{10,14},{3,7},{... | collective-permute-start | bytes 589832 | tf_op jit(solution)/shard_map/ppermute | solution.py:50
  48.5 7.6 %collective-permute-start.14 = (bf16[384,256]{1,0:T(8,128)(2,1)S(1)}, bf16[384,256]{1,0:T(8,128)(2,1)S(1)}, u32[]{:S(2)}, u32[]{:S(2)}) collective-permute-start(bf16[384,256]{1,0:T(8,128)(2,1)S(1)} %collective-permute-done.8), channel_id=1, source_target_pairs={{0,4},{4,8},{8,12},{1,5},{5,9},{9,13},{2,6},{6,10},{10,14},{3,7},{... | collective-permute-start | bytes 589832 | tf_op jit(solution)/shard_map/ppermute | solution.py:50
  52.3 7.1 %collective-permute-start.15 = (bf16[256,640]{0,1:T(8,128)(2,1)S(1)}, bf16[256,640]{0,1:T(8,128)(2,1)S(1)}, u32[]{:S(2)}, u32[]{:S(2)}) collective-permute-start(bf16[256,640]{0,1:T(8,128)(2,1)S(1)} %pad_maximum_fusion.27), channel_id=1, source_target_pairs={{0,1},{1,0},{2,3},{3,2},{4,5},{5,4},{6,7},{7,6},{8,9},{9,8},{10,11... | collective-permute-start | bytes 983048 | tf_op jit(solution)/shard_map/ppermute | solution.py:39
  68.5 13.3 %collective-permute-start.17 = (bf16[384,640]{1,0:T(8,128)(2,1)S(1)}, bf16[384,640]{1,0:T(8,128)(2,1)S(1)}, u32[]{:S(2)}, u32[]{:S(2)}) collective-permute-start(bf16[384,640]{1,0:T(8,128)(2,1)S(1)} %fusion.15), channel_id=1, source_target_pairs={{0,2},{1,3},{2,0},{3,1},{4,6},{5,7},{6,4},{7,5},{8,10},{9,11},{10,... | collective-permute-start | bytes 1474568 | tf_op jit(solution)/shard_map/ppermute | solution.py:44
  89.0 12.7 %collective-permute-start.24 = (bf16[384,640]{1,0:T(8,128)(2,1)}, bf16[384,640]{1,0:T(8,128)(2,1)}, u32[]{:S(2)}, u32[]{:S(2)}) collective-permute-start(bf16[384,640]{1,0:T(8,128)(2,1)} %fusion.17), channel_id=1, source_target_pairs={{0,2},{1,3},{2,0},{3,1},{4,6},{5,7},{6,4},{7,5},{8,10},{9,11},{10,... | collective-permute-start | bytes 1474568 | tf_op jit(solution)/shard_map/ppermute | solution.py:44
  114.0 30.0 %collective-permute-start.26 = (bf16[384,640]{1,0:T(8,128)(2,1)S(1)}, bf16[384,640]{1,0:T(8,128)(2,1)S(1)}, u32[]{:S(2)}, u32[]{:S(2)}) collective-permute-start(bf16[384,640]{1,0:T(8,128)(2,1)S(1)} %fusion.16), channel_id=1, source_target_pairs={{0,2},{1,3},{2,0},{3,1},{4,6},{5,7},{6,4},{7,5},{8,10},{9,11},{10,... | collective-permute-start | bytes 1474568 | tf_op jit(solution)/shard_map/ppermute | solution.py:44
  118.2 25.4 %collective-permute-start.27 = (bf16[640,1024]{1,0:T(8,128)(2,1)S(1)}, bf16[640,1024]{1,0:T(8,128)(2,1)S(1)}, u32[]{:S(2)}, u32[]{:S(2)}) collective-permute-start(bf16[640,1024]{1,0:T(8,128)(2,1)S(1)} %fusion), channel_id=1, source_target_pairs={{0,1},{1,0},{2,3},{3,2},{4,5},{5,4},{6,7},{7,6},{8,9},{9,8},{10,11... | collective-permute-start | bytes 3932168 | tf_op jit(solution)/shard_map/ppermute | solution.py:39
  118.4 13.2 %collective-permute-start.25 = (bf16[384,640]{1,0:T(8,128)(2,1)S(1)}, bf16[384,640]{1,0:T(8,128)(2,1)S(1)}, u32[]{:S(2)}, u32[]{:S(2)}) collective-permute-start(bf16[384,640]{1,0:T(8,128)(2,1)S(1)} %get-tuple-element.153), channel_id=1, source_target_pairs={{0,1},{1,0},{2,3},{3,2},{4,5},{5,4},{6,7},{7,6},{8,9},{9,8},{10,11... | collective-permute-start | bytes 1474568 | tf_op jit(solution)/shard_map/ppermute | solution.py:39
  119.0 9.8 %collective-permute-start.29 = (bf16[320,512]{1,0:T(8,128)(2,1)S(1)}, bf16[320,512]{1,0:T(8,128)(2,1)S(1)}, u32[]{:S(2)}, u32[]{:S(2)}) collective-permute-start(bf16[320,512]{1,0:T(8,128)(2,1)S(1)} %reduce-precision_convert_fusion.9), channel_id=1, source_target_pairs={{0,16},{16,0},{1,17},{17,1},{2,18},{18,2},{3,19},{19,3},{4,20},{20... | collective-permute-start | bytes 983048 | tf_op jit(solution)/shard_map/ppermute | solution.py:95
  140.7 8.1 %collective-permute-start.33 = (bf16[80,512]{1,0:T(8,128)(2,1)S(1)}, bf16[80,512]{1,0:T(8,128)(2,1)S(1)}, u32[]{:S(2)}, u32[]{:S(2)}) collective-permute-start(bf16[80,512]{1,0:T(8,128)(2,1)S(1)} %reduce-precision_convert_fusion.21), channel_id=1, source_target_pairs={{0,8},{4,12},{8,0},{12,4},{1,9},{5,13},{9,1},{13,5},{2,10},{6,14},... | collective-permute-start | bytes 245768 | tf_op jit(solution)/shard_map/ppermute | solution.py:122
  148.9 11.2 %collective-permute-start.64 = (bf16[160,512]{1,0:T(8,128)(2,1)S(1)}, bf16[160,512]{1,0:T(8,128)(2,1)S(1)}, u32[]{:S(2)}, u32[]{:S(2)}) collective-permute-start(bf16[160,512]{1,0:T(8,128)(2,1)S(1)} %pad_maximum_fusion.38), channel_id=1, source_target_pairs={{0,4},{4,0},{8,12},{12,8},{1,5},{5,1},{9,13},{13,9},{2,6},{6,2},{1... | collective-permute-start | bytes 491528 | tf_op jit(solution)/shard_map/ppermute | solution.py:129
  149.4 13.3 %collective-permute-start.32 = (bf16[320,1024]{1,0:T(8,128)(2,1)S(1)}, bf16[320,1024]{1,0:T(8,128)(2,1)S(1)}, u32[]{:S(2)}, u32[]{:S(2)}) collective-permute-start(bf16[320,1024]{1,0:T(8,128)(2,1)S(1)} %reduce-precision_convert_fusion), channel_id=1, source_target_pairs={{0,16},{16,0},{1,17},{17,1},{2,18},{18,2},{3,19},{19,3},{4,20},{20... | collective-permute-start | bytes 1966088 | tf_op jit(solution)/shard_map/ppermute | solution.py:95
  156.7 19.2 %collective-permute-start.38 = (bf16[768,512]{1,0:T(8,128)(2,1)S(1)}, bf16[768,512]{1,0:T(8,128)(2,1)S(1)}, u32[]{:S(2)}, u32[]{:S(2)}) collective-permute-start(bf16[768,512]{1,0:T(8,128)(2,1)S(1)} %pad_maximum_fusion.12), channel_id=1, source_target_pairs={{0,1},{1,0},{2,3},{3,2},{4,5},{5,4},{6,7},{7,6},{8,9},{9,8},{10,11... | collective-permute-start | bytes 2359304 | tf_op jit(solution)/shard_map/ppermute | solution.py:39
  165.1 9.2 %collective-permute-start.35 = (bf16[160,1024]{1,0:T(8,128)(2,1)S(1)}, bf16[160,1024]{1,0:T(8,128)(2,1)S(1)}, u32[]{:S(2)}, u32[]{:S(2)}) collective-permute-start(bf16[160,1024]{1,0:T(8,128)(2,1)S(1)} %reduce-precision_convert_fusion.8), channel_id=1, source_target_pairs={{0,4},{4,0},{8,12},{12,8},{1,5},{5,1},{9,13},{13,9},{2,6},{6,2},{1... | collective-permute-start | bytes 983048 | tf_op jit(solution)/shard_map/ppermute | solution.py:106
  170.5 13.3 %collective-permute-start.40 = (bf16[640,512]{1,0:T(8,128)(2,1)S(1)}, bf16[640,512]{1,0:T(8,128)(2,1)S(1)}, u32[]{:S(2)}, u32[]{:S(2)}) collective-permute-start(bf16[640,512]{1,0:T(8,128)(2,1)S(1)} %fusion.9), channel_id=1, source_target_pairs={{0,1},{1,0},{2,3},{3,2},{4,5},{5,4},{6,7},{7,6},{8,9},{9,8},{10,11... | collective-permute-start | bytes 1966088 | tf_op jit(solution)/shard_map/ppermute | solution.py:39
  170.8 24.0 %collective-permute-start.34 = (bf16[768,512]{1,0:T(8,128)(2,1)S(1)}, bf16[768,512]{1,0:T(8,128)(2,1)S(1)}, u32[]{:S(2)}, u32[]{:S(2)}) collective-permute-start(bf16[768,512]{1,0:T(8,128)(2,1)S(1)} %pad_maximum_fusion.11), channel_id=1, source_target_pairs={{0,1},{1,0},{2,3},{3,2},{4,5},{5,4},{6,7},{7,6},{8,9},{9,8},{10,11... | collective-permute-start | bytes 2359304 | tf_op jit(solution)/shard_map/ppermute | solution.py:39
  174.4 9.2 %collective-permute-start.36 = (bf16[80,1024]{1,0:T(8,128)(2,1)S(1)}, bf16[80,1024]{1,0:T(8,128)(2,1)S(1)}, u32[]{:S(2)}, u32[]{:S(2)}) collective-permute-start(bf16[80,1024]{1,0:T(8,128)(2,1)S(1)} %reduce-precision_convert_fusion.12), channel_id=1, source_target_pairs={{0,8},{4,12},{8,0},{12,4},{1,9},{5,13},{9,1},{13,5},{2,10},{6,14},... | collective-permute-start | bytes 491528 | tf_op jit(solution)/shard_map/ppermute | solution.py:116
  176.2 15.8 %collective-permute-start.39 = (bf16[2,192,512]{2,1,0:T(8,128)(2,1)S(1)}, bf16[2,192,512]{2,1,0:T(8,128)(2,1)S(1)}, u32[]{:S(2)}, u32[]{:S(2)}) collective-permute-start(bf16[2,192,512]{2,1,0:T(8,128)(2,1)S(1)} %reduce-precision_convert_fusion.4), channel_id=1, source_target_pairs={{0,2},{1,3},{2,0},{3,1},{4,6},{5,7},{6,4},{7,5},{8,10},{9,11},{10,... | collective-permute-start | bytes 1179656 | tf_op jit(solution)/shard_map/ppermute | solution.py:44
  183.7 8.1 %collective-permute-start.46 = (bf16[80,1024]{1,0:T(8,128)(2,1)S(1)}, bf16[80,1024]{1,0:T(8,128)(2,1)S(1)}, u32[]{:S(2)}, u32[]{:S(2)}) collective-permute-start(bf16[80,1024]{1,0:T(8,128)(2,1)S(1)} %reduce-precision_convert_fusion.11), channel_id=1, source_target_pairs={{0,8},{4,12},{8,0},{12,4},{1,9},{5,13},{9,1},{13,5},{2,10},{6,14},... | collective-permute-start | bytes 491528 | tf_op jit(solution)/shard_map/ppermute | solution.py:122
  184.0 12.4 %collective-permute-start.45 = (bf16[320,512]{1,0:T(8,128)(2,1)S(1)}, bf16[320,512]{1,0:T(8,128)(2,1)S(1)}, u32[]{:S(2)}, u32[]{:S(2)}) collective-permute-start(bf16[320,512]{1,0:T(8,128)(2,1)S(1)} %reduce-precision_convert_fusion.7), channel_id=1, source_target_pairs={{0,16},{16,0},{1,17},{17,1},{2,18},{18,2},{3,19},{19,3},{4,20},{20... | collective-permute-start | bytes 983048 | tf_op jit(solution)/shard_map/ppermute | solution.py:95
  191.9 17.6 %collective-permute-start.63 = (bf16[160,1024]{1,0:T(8,128)(2,1)S(1)}, bf16[160,1024]{1,0:T(8,128)(2,1)S(1)}, u32[]{:S(2)}, u32[]{:S(2)}) collective-permute-start(bf16[160,1024]{1,0:T(8,128)(2,1)S(1)} %pad_maximum_fusion.28), channel_id=1, source_target_pairs={{0,4},{4,0},{8,12},{12,8},{1,5},{5,1},{9,13},{13,9},{2,6},{6,2},{1... | collective-permute-start | bytes 983048 | tf_op jit(solution)/shard_map/ppermute | solution.py:129
  192.1 17.6 %collective-permute-start.41 = (bf16[192,512]{1,0:T(8,128)(2,1)S(1)}, bf16[192,512]{1,0:T(8,128)(2,1)S(1)}, u32[]{:S(2)}, u32[]{:S(2)}) collective-permute-start(bf16[192,512]{1,0:T(8,128)(2,1)S(1)} %get-tuple-element.163), channel_id=1, source_target_pairs={{12,0},{13,1},{14,2},{15,3},{28,16},{29,17},{30,18},{31,19}} | collective-permute-start | bytes 589832 | tf_op jit(solution)/shard_map/ppermute | solution.py:50
  193.4 19.1 %collective-permute-start.43 = (bf16[192,512]{1,0:T(8,128)(2,1)S(1)}, bf16[192,512]{1,0:T(8,128)(2,1)S(1)}, u32[]{:S(2)}, u32[]{:S(2)}) collective-permute-start(bf16[192,512]{1,0:T(8,128)(2,1)S(1)} %get-tuple-element.162), channel_id=1, source_target_pairs={{8,0},{12,4},{9,1},{13,5},{10,2},{14,6},{11,3},{15,7},{24,16},{28,... | collective-permute-start | bytes 589832 | tf_op jit(solution)/shard_map/ppermute | solution.py:50
  195.1 14.7 %collective-permute-start.37 = (bf16[2,192,512]{2,1,0:T(8,128)(2,1)S(1)}, bf16[2,192,512]{2,1,0:T(8,128)(2,1)S(1)}, u32[]{:S(2)}, u32[]{:S(2)}) collective-permute-start(bf16[2,192,512]{2,1,0:T(8,128)(2,1)S(1)} %reduce-precision_convert_fusion.5), channel_id=1, source_target_pairs={{0,2},{1,3},{2,0},{3,1},{4,6},{5,7},{6,4},{7,5},{8,10},{9,11},{10,... | collective-permute-start | bytes 1179656 | tf_op jit(solution)/shard_map/ppermute | solution.py:44
  210.0 8.0 %collective-permute-start.44 = (bf16[192,512]{1,0:T(8,128)(2,1)S(1)}, bf16[192,512]{1,0:T(8,128)(2,1)S(1)}, u32[]{:S(2)}, u32[]{:S(2)}) collective-permute-start(bf16[192,512]{1,0:T(8,128)(2,1)S(1)} %fusion.69), channel_id=1, source_target_pairs={{4,0},{8,4},{12,8},{5,1},{9,5},{13,9},{6,2},{10,6},{14,10},{7,3},{... | collective-permute-start | bytes 589832 | tf_op jit(solution)/shard_map/ppermute | solution.py:50
  211.6 17.7 %collective-permute-start.42 = (bf16[384,640]{1,0:T(8,128)(2,1)S(1)}, bf16[384,640]{1,0:T(8,128)(2,1)S(1)}, u32[]{:S(2)}, u32[]{:S(2)}) collective-permute-start(bf16[384,640]{1,0:T(8,128)(2,1)S(1)} %reduce-precision_convert_fusion.2), channel_id=1, source_target_pairs={{0,2},{1,3},{2,0},{3,1},{4,6},{5,7},{6,4},{7,5},{8,10},{9,11},{10,... | collective-permute-start | bytes 1474568 | tf_op jit(solution)/shard_map/ppermute | solution.py:44
  220.9 8.4 %collective-permute-start.47 = (bf16[192,640]{1,0:T(8,128)(2,1)S(1)}, bf16[192,640]{1,0:T(8,128)(2,1)S(1)}, u32[]{:S(2)}, u32[]{:S(2)}) collective-permute-start(bf16[192,640]{1,0:T(8,128)(2,1)S(1)} %get-tuple-element.85), channel_id=1, source_target_pairs={{0,2},{1,3},{2,0},{3,1},{4,6},{5,7},{6,4},{7,5},{8,10},{9,11},{10,... | collective-permute-start | bytes 737288 | tf_op jit(solution)/shard_map/ppermute | solution.py:44
  223.0 7.3 %collective-permute-start.49 = (bf16[672,256]{1,0:T(8,128)(2,1)S(1)}, bf16[672,256]{1,0:T(8,128)(2,1)S(1)}, u32[]{:S(2)}, u32[]{:S(2)}) collective-permute-start(bf16[672,256]{1,0:T(8,128)(2,1)S(1)} %reduce-precision_convert_fusion.6), channel_id=1, source_target_pairs={{0,1},{1,0},{2,3},{3,2},{4,5},{5,4},{6,7},{7,6},{8,9},{9,8},{10,11... | collective-permute-start | bytes 1032200 | tf_op jit(solution)/shard_map/ppermute | solution.py:39
  230.2 29.8 %collective-permute-start.48 = (bf16[384,640]{1,0:T(8,128)(2,1)S(1)}, bf16[384,640]{1,0:T(8,128)(2,1)S(1)}, u32[]{:S(2)}, u32[]{:S(2)}) collective-permute-start(bf16[384,640]{1,0:T(8,128)(2,1)S(1)} %reduce-precision_convert_fusion.1), channel_id=1, source_target_pairs={{0,1},{1,0},{2,3},{3,2},{4,5},{5,4},{6,7},{7,6},{8,9},{9,8},{10,11... | collective-permute-start | bytes 1474568 | tf_op jit(solution)/shard_map/ppermute | solution.py:39
  236.3 9.6 %collective-permute-start.61 = (bf16[80,512]{1,0:T(8,128)(2,1)S(1)}, bf16[80,512]{1,0:T(8,128)(2,1)S(1)}, u32[]{:S(2)}, u32[]{:S(2)}) collective-permute-start(bf16[80,512]{1,0:T(8,128)(2,1)S(1)} %reduce-precision_convert_fusion.19), channel_id=1, source_target_pairs={{0,8},{4,12},{8,0},{12,4},{1,9},{5,13},{9,1},{13,5},{2,10},{6,14},... | collective-permute-start | bytes 245768 | tf_op jit(solution)/shard_map/ppermute | solution.py:122
  239.7 9.5 %collective-permute-start.55 = (bf16[336,128]{1,0:T(8,128)(2,1)S(1)}, bf16[336,128]{1,0:T(8,128)(2,1)S(1)}, u32[]{:S(2)}, u32[]{:S(2)}) collective-permute-start(bf16[336,128]{1,0:T(8,128)(2,1)S(1)} %reduce-precision_convert_fusion.15), channel_id=1, source_target_pairs={{0,8},{4,12},{8,0},{12,4},{1,9},{5,13},{9,1},{13,5},{2,10},{6,14},... | collective-permute-start | bytes 258056 | tf_op jit(solution)/shard_map/ppermute | solution.py:138
  241.4 7.8 %collective-permute-start.56 = (bf16[336,128]{1,0:T(8,128)(2,1)S(1)}, bf16[336,128]{1,0:T(8,128)(2,1)S(1)}, u32[]{:S(2)}, u32[]{:S(2)}) collective-permute-start(bf16[336,128]{1,0:T(8,128)(2,1)S(1)} %reduce-precision_convert_fusion.15), channel_id=1, source_target_pairs={{0,4},{4,8},{8,12},{12,0},{1,5},{5,9},{9,13},{13,1},{2,6},{6,10},{... | collective-permute-start | bytes 258056 | tf_op jit(solution)/shard_map/ppermute | solution.py:138
  251.0 8.0 %collective-permute-start.62 = (bf16[160,512]{1,0:T(8,128)(2,1)S(1)}, bf16[160,512]{1,0:T(8,128)(2,1)S(1)}, u32[]{:S(2)}, u32[]{:S(2)}) collective-permute-start(bf16[160,512]{1,0:T(8,128)(2,1)S(1)} %pad_maximum_fusion.39), channel_id=1, source_target_pairs={{0,4},{4,0},{8,12},{12,8},{1,5},{5,1},{9,13},{13,9},{2,6},{6,2},{1... | collective-permute-start | bytes 491528 | tf_op jit(solution)/shard_map/ppermute | solution.py:129
  (97 other events, 550.5 us)
